TPU v7x, 256 devices: a whole 4x4x8 slice. The times are simulated.
256 devices in a mesh: rep: 32 (over y, z), tp: 8 (over x, core).
Axes of the slice: x: 4, y: 4, z: 8, core: 2. Of those that a mesh axis runs over, the one named last changes fastest.
Arguments:
- reference_rows: bfloat16 [32768, 8192], P('rep', 'tp'), may hold values from -7 to 7
- critic_rows: bfloat16 [32768, 4096], P('rep', 'tp'), may hold values from -7 to 7
- segment_ids: int32 [32768], P('rep'), may hold values from -1 to 32767, as said below
- pack_dest: int32 [32, 32], P('rep'), may hold values from 0 to 31, as said below
- ref_query: bfloat16 [8192, 4096], P('rep', 'tp'), may hold values from -2 to 2
- ref_key: bfloat16 [8192, 1024], P('rep', 'tp'), may hold values from -2 to 2
- ref_value: bfloat16 [8192, 1024], P('rep', 'tp'), may hold values from -0.0625 to 0.0625
- critic_query: bfloat16 [4096, 4096], P(None, 'tp'), may hold values from -2 to 2
- critic_key: bfloat16 [4096, 1024], P(None, 'tp'), may hold values from -2 to 2
- critic_value: bfloat16 [4096, 1024], P(None, 'tp'), may hold values from -0.09375 to 0.09375
- ref_readout: bfloat16 [4096], P('tp'), may hold values from -0.09375 to 0.09375
- critic_readout: bfloat16 [4096], P('tp'), may hold values from -0.09375 to 0.09375
Outputs:
- ref_score: float32 [32768], P('rep')
- value: float32 [32768], P('rep')
Inputs may be any that keep to these rules, and one draw needn't show every extreme that they name: Each row is a permutation: block b of replica s goes to pack pack_dest[s, b]. `segment_ids`: in every aligned block of 32 slots the used rows come first and the rest hold -1; a block holds 1 to 31 used rows, and every pack receives exactly 31 used rows from some replica and exactly 512 used rows in all. A rollout is a run of consecutive used rows with one id inside one block; different rollouts have different ids.
All inputs are finite; a program needn't handle non-finite values.
Results may differ from a plain program's by a relative error of at most 0.0084.
Values may be sent and summed in bfloat16 or wider, within the bound.
No kernel may reach another device: no remote copies, remote signals or barrier semaphores. Data moves between devices by JAX's collectives and lax.ppermute only.
A program may use at most 128 MiB of HBM per device.

v0:
```python
import jax
import jax.numpy as jnp
from jax import lax
from jax.sharding import PartitionSpec as P

HD = 128


def normalize(source):
    widened = source.astype(jnp.float32)
    scale_row = lax.rsqrt(jnp.mean(widened * widened, axis=-1, keepdims=True) + 1e-05)
    return (widened * scale_row).astype(jnp.bfloat16)


def attend(queries, keys_in, values_in, segments):
    row_count = queries.shape[0]
    groups = keys_in.shape[1] // HD
    shared = queries.shape[1] // keys_in.shape[1]
    query_four = queries.reshape(row_count, groups, shared, HD)
    key_three = keys_in.reshape(row_count, groups, HD)
    value_three = values_in.reshape(row_count, groups, HD)
    scores = jnp.einsum(
        "pgjd,qgd->gjpq", query_four, key_three, preferred_element_type=jnp.float32
    ) * HD ** (-0.5)
    position = jnp.arange(row_count)
    allowed = (position[None, :] <= position[:, None]) & (segments[:, None] == segments[None, :])
    masked = jnp.where(allowed, scores, -1e30)
    row_max = jnp.max(masked, axis=-1, keepdims=True)
    powers = jnp.where(allowed, jnp.exp(masked - row_max), 0.0)
    weights = (powers / jnp.sum(powers, axis=-1, keepdims=True)).astype(jnp.bfloat16)
    mixture = jnp.einsum("gjpq,qgd->pgjd", weights, value_three, preferred_element_type=jnp.float32)
    return mixture.reshape(row_count, groups * shared * HD).astype(jnp.bfloat16)


def compact_index(segments):
    row_count = segments.shape[0]
    sort_keys = jnp.where(segments >= 0, 0, row_count).astype(jnp.int32) + jnp.arange(
        row_count, dtype=jnp.int32
    )
    return jnp.argsort(sort_keys)[: row_count // 2]


def project(normed, weight):
    return jnp.dot(normed, weight, preferred_element_type=jnp.float32).astype(jnp.bfloat16)


def body(
    reference_rows,
    critic_rows,
    segment_ids,
    pack_dest,
    ref_query,
    ref_key,
    ref_value,
    critic_query,
    critic_key,
    critic_value,
    ref_readout,
    critic_readout,
):
    replicas = lax.axis_size("rep")
    slot_count = segment_ids.shape[0]
    block_rows = slot_count // replicas
    destination = pack_dest[0]
    inverse = jnp.argsort(destination)

    def by_pack(source):
        blocks = source.reshape((replicas, block_rows) + source.shape[1:])
        return jnp.take(blocks, inverse, axis=0).reshape(source.shape)

    ref_in, critic_in, ids_in = (
        lax.all_to_all(by_pack(reference_rows), "rep", split_axis=0, concat_axis=0, tiled=True),
        lax.all_to_all(by_pack(critic_rows), "rep", split_axis=0, concat_axis=0, tiled=True),
        lax.all_to_all(by_pack(segment_ids), "rep", split_axis=0, concat_axis=0, tiled=True),
    )
    chosen = compact_index(ids_in)
    pack_ids = ids_in[chosen]
    ref_full, critic_full = (
        lax.all_gather(ref_in[chosen], "tp", axis=1, tiled=True),
        lax.all_gather(critic_in[chosen], "tp", axis=1, tiled=True),
    )
    critic_normed = normalize(critic_full)
    critic_attn = attend(
        project(critic_normed, critic_query),
        project(critic_normed, critic_key),
        project(critic_normed, critic_value),
        pack_ids,
    )
    ref_normed = normalize(ref_full)
    pieces = (
        lax.all_gather(ref_query, "rep", axis=0, tiled=True),
        lax.all_gather(ref_key, "rep", axis=0, tiled=True),
        lax.all_gather(ref_value, "rep", axis=0, tiled=True),
    )
    ref_q, ref_k, ref_v = tuple(
        (
            jnp.dot(ref_normed, weight_piece, preferred_element_type=jnp.float32)
            for weight_piece in pieces
        )
    )
    ref_attn = attend(
        ref_q.astype(jnp.bfloat16), ref_k.astype(jnp.bfloat16), ref_v.astype(jnp.bfloat16), pack_ids
    )
    ref_spread = jnp.zeros((slot_count, ref_attn.shape[1]), jnp.bfloat16).at[chosen].set(ref_attn)
    critic_spread = (
        jnp.zeros((slot_count, critic_attn.shape[1]), jnp.bfloat16).at[chosen].set(critic_attn)
    )
    ref_home, critic_home = (
        lax.all_to_all(ref_spread, "rep", split_axis=0, concat_axis=0, tiled=True),
        lax.all_to_all(critic_spread, "rep", split_axis=0, concat_axis=0, tiled=True),
    )
    ref_home = jnp.take(ref_home.reshape(replicas, block_rows, -1), destination, axis=0).reshape(
        slot_count, -1
    )
    critic_home = jnp.take(
        critic_home.reshape(replicas, block_rows, -1), destination, axis=0
    ).reshape(slot_count, -1)
    partial_value = jnp.stack(
        [
            jnp.dot(ref_home, ref_readout, preferred_element_type=jnp.float32),
            jnp.dot(critic_home, critic_readout, preferred_element_type=jnp.float32),
        ]
    )
    ordered = lax.psum(partial_value, "tp")
    ordered = jnp.where(segment_ids[None, :] >= 0, ordered, 0.0)
    return (ordered[0], ordered[1])


def solution(mesh):
    return jax.shard_map(
        body,
        mesh=mesh,
        in_specs=(
            P("rep", "tp"),
            P("rep", "tp"),
            P("rep"),
            P("rep", None),
            P("rep", "tp"),
            P("rep", "tp"),
            P("rep", "tp"),
            P(None, "tp"),
            P(None, "tp"),
            P(None, "tp"),
            P("tp"),
            P("tp"),
        ),
        out_specs=(P("rep"), P("rep")),
        check_vma=False,
    )
```

profile of v0, /device:TPU:1, one launch (start us, length us, event | category | flops | bytes accessed | tf_op | source)
XLA Modules:
  0.0 513.9 jit_solution(6631517655676095522)
XLA Ops:
  7.2 2.4 sort.34
  9.6 0.8 reshape.165
  10.4 0.6 gather_fusion
  10.9 0.7 bitcast_select_fusion.2
  11.6 12.0 %all-to-all-start = ((s32[32,32,1]{1,2,0:T(1,128)}), s32[32,32,1]{1,2,0:T(1,128)S(1)}, u32[]{:S(2)}, u32[]{:S(2)}) async-start(s32[32,32,1]{1,2,0:T(1,128)} %bitcast.2), calls=%async_computation | async-start | bytes 32768 | tf_op jit(solution)/shard_map/all_to_all | solution.py:74
  23.7 1.8 gather_fusion.6
  25.5 1.2 broadcast_select_fusion.1
  26.7 5.6 %all-to-all-done = s32[32,32,1]{1,2,0:T(1,128)S(1)} async-done(((s32[32,32,1]{1,2,0:T(1,128)}), s32[32,32,1]{1,2,0:T(1,128)S(1)}, u32[]{:S(2)}, u32[]{:S(2)}) %all-to-all-start) | async-done | bytes 4128 | tf_op jit(solution)/shard_map/all_to_all | solution.py:74
  32.3 3.9 all-to-all-start.3
  36.3 0.5 broadcast.155
  36.8 0.7 reduce.7
  37.6 4.4 sort.35
  41.9 18.7 %all-to-all-done.3 = bf16[32,32,512]{2,1,0:T(8,128)(2,1)S(1)} async-done(((bf16[32,32,512]{2,1,0:T(8,128)(2,1)}), bf16[32,32,512]{2,1,0:T(8,128)(2,1)S(1)}, u32[]{:S(2)}, u32[]{:S(2)}) %all-to-all-start.3) | async-done | bytes 1048608 | tf_op jit(solution)/shard_map/all_to_all | solution.py:73
  60.6 2.6 gather_fusion.4
  63.3 2.0 gather_fusion.1
  65.4 1.8 broadcast_select_fusion
  67.2 55.1 %all_to_all.45 = bf16[32,32,1024]{2,1,0:T(8,128)(2,1)} all-to-all(bf16[32,32,1024]{2,1,0:T(8,128)(2,1)S(1)} %broadcast_select_fusion), channel_id=1, replica_groups=mesh['rep'=32,'tp'=8] {'rep'}, dimensions={0} | all-to-all | bytes 4194304 | tf_op jit(solution)/shard_map/all_to_all | solution.py:72
  122.3 5.4 %gather_fusion.2 = bf16[512,1024]{1,0:T(8,128)(2,1)} fusion(bf16[1024,1024]{1,0:T(8,128)(2,1)} %bitcast.109, s32[1024]{0:T(1024)S(1)} %pad_clamp_fusion.1), kind=kCustom, calls=%fused_computation.5 | custom fusion | bytes 2099200 | tf_op jit(solution)/shard_map/gather | solution.py:79
  127.7 0.7 all-gather.12.cloned.1.call-update
  128.5 0.5 all-gather.10.cloned.1.call-update
  129.0 0.5 all-gather.8.cloned.1.call-update
  129.6 2.5 gather_fusion.3
  132.3 3.2 fusion.2
  135.8 4.7 convolution_convert_fusion
  140.5 41.1 %all-gather.14.cloned.1.call-done = bf16[512,8192]{1,0:T(8,128)(2,1)} async-done(((bf16[512,1024]{1,0:T(8,128)(2,1)}), bf16[512,8192]{1,0:T(8,128)(2,1)}) %all-gather.14.cloned.1.call-update) | async-done | bytes 8388624 | tf_op jit(solution)/shard_map/all_gather | solution.py:79
  181.5 5.1 fusion
  186.6 95.4 %all-gather.12.cloned.1.call-done = bf16[8192,512]{1,0:T(8,128)(2,1)} async-done(((bf16[256,512]{1,0:T(8,128)(2,1)}), bf16[8192,512]{1,0:T(8,128)(2,1)}) %all-gather.12.cloned.1.call-update) | async-done | bytes 8388624 | tf_op jit(solution)/shard_map/all_gather | solution.py:91
  282.1 11.2 %convolution_convert_fusion.1 = bf16[512,512]{0,1:T(8,128)(2,1)} fusion(bf16[8192,512]{1,0:T(8,128)(2,1)} %all-gather.12.cloned.1.call-done, bf16[512,8192]{1,0:T(8,128)(2,1)} %all-gather.14.cloned.1.call-done, f32[512]{0:T(512)S(1)} %add_rsqrt_fusion.1), kind=kOutput, calls=%fused_computation.38 | convolution fusion | flops 4307812352 | bytes 17303552 | tf_op jit(solution)/shard_map/dot_general | solution.py:97
  293.3 62.8 %all-gather.10.cloned.1.call-done = bf16[8192,128]{1,0:T(8,128)(2,1)} async-done(((bf16[256,128]{1,0:T(8,128)(2,1)}), bf16[8192,128]{1,0:T(8,128)(2,1)}) %all-gather.10.cloned.1.call-update) | async-done | bytes 2097168 | tf_op jit(solution)/shard_map/all_gather | solution.py:92
  356.1 10.2 %fusion.4 = (f32[4,512]{1,0:T(4,128)S(1)}, f32[512,512,4]{1,0,2:T(8,128)}) fusion(pred[512,512]{0,1:T(8,128)(4,1)S(1)} %fusion.26, bf16[512,4,128]{0,2,1:T(8,128)(2,1)} %bitcast.122, bf16[8192,128]{1,0:T(8,128)(2,1)} %all-gather.10.cloned.1.call-done, bf16[512,8192]{1,0:T(8,128)(2,1)} %all-gather.14.cloned.1.call-done, f32[512]{0:T(512)S(1)} %add_rsqrt_fusion.1), kind=kOutput, calls=%fused_computation.24 | convolution fusion | flops 1357969408 | bytes 15476736 | tf_op jit(solution)/shard_map/pgjd,qgd->gjpq/dot_general | solution.py:22
  366.3 9.5 %fusion.6 = (f32[4,512]{1,0:T(4,128)S(1)}, f32[4,512]{1,0:T(4,128)S(1)}, f32[512,512,4]{1,0,2:T(8,128)}) fusion(f32[512,512,4]{1,0,2:T(8,128)} %get-tuple-element.14, f32[4,512]{1,0:T(4,128)S(1)} %get-tuple-element.13, pred[512,512]{0,1:T(8,128)(4,1)S(1)} %fusion.26, bf16[512,4,128]{0,2,1:T(8,128)(2,1)S(1)} %bitcast.121, bf16[4096,128]{1,0:T(8,128)(2,1)} %param.22, ...), kind=kOutput, calls=%fused_computation.26 | convolution fusion | flops 820047872 | bytes 14444544 | tf_op jit(solution)/shard_map/pgjd,qgd->gjpq/dot_general | solution.py:22
  375.8 3.2 fusion.7
  379.0 6.6 %fusion.17 = bf16[128,4,512]{2,0,1:T(8,128)(2,1)S(1)} fusion(f32[4,512]{1,0:T(4,128)S(1)} %fusion.7, f32[4,512]{1,0:T(4,128)S(1)} %get-tuple-element.8, f32[512,512,4]{1,0,2:T(8,128)} %get-tuple-element.15, pred[512,512]{0,1:T(8,128)(4,1)S(1)} %fusion.26, bf16[4096,128]{1,0:T(8,128)(2,1)} %param.23, bf16[512,4096]{1,0:T(8,128)(2,1)} %all-gather.16.cloned.1.call-done, ...), kind=kOutput, calls=%fused_computation.37 | convolution fusion | flops 818216960 | bytes 10242048 | tf_op jit(solution)/shard_map/gjpq,qgd->pgjd/dot_general | solution.py:31
  385.9 3.5 scatter_custom_fusion.1
  389.4 5.3 %all-to-all-start.4 = ((bf16[32,32,512]{2,1,0:T(8,128)(2,1)}), bf16[32,32,512]{2,1,0:T(8,128)(2,1)S(1)}, u32[]{:S(2)}, u32[]{:S(2)}) async-start(bf16[32,32,512]{2,1,0:T(8,128)(2,1)} %bitcast.113), calls=%async_computation.4 | async-start | bytes 2097152 | tf_op jit(solution)/shard_map/all_to_all | solution.py:110
  394.8 42.2 %all-gather.8.cloned.1.call-done = bf16[8192,128]{1,0:T(8,128)(2,1)} async-done(((bf16[256,128]{1,0:T(8,128)(2,1)}), bf16[8192,128]{1,0:T(8,128)(2,1)}) %all-gather.8.cloned.1.call-update) | async-done | bytes 2097168 | tf_op jit(solution)/shard_map/all_gather | solution.py:93
  437.0 9.9 %fusion.14 = bf16[128,4,512]{2,0,1:T(8,128)(2,1)} fusion(f32[4,512]{1,0:T(4,128)S(1)} %get-tuple-element.7, f32[4,512]{1,0:T(4,128)S(1)} %get-tuple-element.13, f32[512,512,4]{1,0,2:T(8,128)} %get-tuple-element.14, pred[512,512]{0,1:T(8,128)(4,1)S(1)} %fusion.26, bf16[8192,128]{1,0:T(8,128)(2,1)} %all-gather.8.cloned.1.call-done, ...), kind=kOutput, calls=%fused_computation.36 | convolution fusion | flops 1361379328 | bytes 15484928 | tf_op jit(solution)/shard_map/gjpq,qgd->pgjd/dot_general | solution.py:31
  446.9 2.1 copy.28
  449.0 4.0 scatter_custom_fusion
  453.0 6.6 %all-to-all-start.2 = ((bf16[32,32,512]{2,1,0:T(8,128)(2,1)}), bf16[32,32,512]{2,1,0:T(8,128)(2,1)}, u32[]{:S(2)}, u32[]{:S(2)}) async-start(bf16[32,32,512]{2,1,0:T(8,128)(2,1)} %bitcast.114), calls=%async_computation.2 | async-start | bytes 2097152 | tf_op jit(solution)/shard_map/all_to_all | solution.py:109
  459.7 1.8 gather_fusion.7
  461.6 19.6 %all-to-all-done.2 = bf16[32,32,512]{2,1,0:T(8,128)(2,1)} async-done(((bf16[32,32,512]{2,1,0:T(8,128)(2,1)}), bf16[32,32,512]{2,1,0:T(8,128)(2,1)}, u32[]{:S(2)}, u32[]{:S(2)}) %all-to-all-start.2) | async-done | bytes 1048608 | tf_op jit(solution)/shard_map/all_to_all | solution.py:109
  481.1 2.8 gather_fusion.5
  484.0 1.5 broadcast_select_fusion.3
  485.5 0.4 fusion.52
  485.8 0.4 fusion.53
  486.2 20.0 %psum.7 = f32[2,1024]{1,0:T(2,128)S(1)} all-reduce(f32[2,1024]{1,0:T(2,128)S(1)} %pad_maximum_fusion), channel_id=1, replica_groups=mesh['rep'=32,'tp'=8] {'tp'}, use_global_device_ids=true, to_apply=%region_10.12 | all-reduce | flops 2048 | bytes 16384 | tf_op jit(solution)/shard_map/psum | solution.py:124
  506.3 0.6 fusion.47
  (44 shorter events, 1.1 us)
Async XLA Ops:
  7.2 56.2 %copy-start = (bf16[1024,1024]{1,0:T(8,128)(2,1)S(1)}, bf16[1024,1024]{1,0:T(8,128)(2,1)}, u32[]{:S(2)}) copy-start(bf16[1024,1024]{1,0:T(8,128)(2,1)} %param.14) | copy-start | bytes 6291460
  11.6 20.7 %all-to-all-start = ((s32[32,32,1]{1,2,0:T(1,128)}), s32[32,32,1]{1,2,0:T(1,128)S(1)}, u32[]{:S(2)}, u32[]{:S(2)}) async-start(s32[32,32,1]{1,2,0:T(1,128)} %bitcast.2), calls=%async_computation | async-start | bytes 32768 | tf_op jit(solution)/shard_map/all_to_all | solution.py:74
  32.3 28.3 %all-to-all-start.3 = ((bf16[32,32,512]{2,1,0:T(8,128)(2,1)}), bf16[32,32,512]{2,1,0:T(8,128)(2,1)S(1)}, u32[]{:S(2)}, u32[]{:S(2)}) async-start(bf16[32,32,512]{2,1,0:T(8,128)(2,1)} %broadcast_select_fusion.1), calls=%async_computation.3 | async-start | bytes 2097152 | tf_op jit(solution)/shard_map/all_to_all | solution.py:73
  36.2 96.1 %all-gather.16.cloned.1.call-start = ((), (), s32[]{:S(2)}) async-start(), calls=%async_computation.9 | async-start | bytes 4718592 | tf_op jit(solution)/shard_map/all_gather | solution.py:80
  63.3 118.3 %all-gather.14.cloned.1.call-start = ((), (), s32[]{:S(2)}) async-start(), calls=%async_computation.8 | async-start | bytes 9437184 | tf_op jit(solution)/shard_map/all_gather | solution.py:79
  127.7 154.4 %all-gather.12.cloned.1.call-start = ((), (), s32[]{:S(2)}) async-start(), calls=%async_computation.7 | async-start | bytes 8650752 | tf_op jit(solution)/shard_map/all_gather | solution.py:91
  128.4 227.6 %all-gather.10.cloned.1.call-start = ((), (), s32[]{:S(2)}) async-start(), calls=%async_computation.6 | async-start | bytes 2162688 | tf_op jit(solution)/shard_map/all_gather | solution.py:92
  129.0 308.0 %all-gather.8.cloned.1.call-start = ((), (), s32[]{:S(2)}) async-start(), calls=%async_computation.5 | async-start | bytes 2162688 | tf_op jit(solution)/shard_map/all_gather | solution.py:93
  132.3 3.5 copy-start.2
  389.4 63.6 %all-to-all-start.4 = ((bf16[32,32,512]{2,1,0:T(8,128)(2,1)}), bf16[32,32,512]{2,1,0:T(8,128)(2,1)S(1)}, u32[]{:S(2)}, u32[]{:S(2)}) async-start(bf16[32,32,512]{2,1,0:T(8,128)(2,1)} %bitcast.113), calls=%async_computation.4 | async-start | bytes 2097152 | tf_op jit(solution)/shard_map/all_to_all | solution.py:110
  446.9 12.7 %copy-start.4 = (bf16[512]{0:T(512)(128)(2,1)S(1)}, bf16[512]{0:T(512)(128)(2,1)}, u32[]{:S(2)}) copy-start(bf16[512]{0:T(512)(128)(2,1)} %param.24) | copy-start | bytes 3076
  446.9 12.7 %copy-start.5 = (bf16[512]{0:T(512)(128)(2,1)S(1)}, bf16[512]{0:T(512)(128)(2,1)}, u32[]{:S(2)}) copy-start(bf16[512]{0:T(512)(128)(2,1)} %param.25) | copy-start | bytes 3076
  446.9 12.8 %copy-start.6 = (s32[1,32]{1,0:T(1,128)S(1)}, s32[1,32]{1,0:T(1,128)}, u32[]{:S(2)}) copy-start(s32[1,32]{1,0:T(1,128)} %param.17) | copy-start | bytes 388
  446.9 12.8 %copy-start.3 = (s32[1024]{0:T(1024)S(1)}, s32[1024]{0:T(1024)}, u32[]{:S(2)}) copy-start(s32[1024]{0:T(1024)} %param.16) | copy-start | bytes 12292
  453.0 6.7 %copy-start.1 = (bf16[32,32,512]{2,1,0:T(8,128)(2,1)}, bf16[32,32,512]{2,1,0:T(8,128)(2,1)S(1)}, u32[]{:S(2)}) copy-start(bf16[32,32,512]{2,1,0:T(8,128)(2,1)S(1)} %all-to-all-done.4) | copy-start | bytes 3145732
  453.0 28.2 %all-to-all-start.2 = ((bf16[32,32,512]{2,1,0:T(8,128)(2,1)}), bf16[32,32,512]{2,1,0:T(8,128)(2,1)}, u32[]{:S(2)}, u32[]{:S(2)}) async-start(bf16[32,32,512]{2,1,0:T(8,128)(2,1)} %bitcast.114), calls=%async_computation.2 | async-start | bytes 2097152 | tf_op jit(solution)/shard_map/all_to_all | solution.py:109
Sparse Core Ops, SparseCore 0:
  63.4 36.1 all-gather.15
  127.8 53.6 all-gather.13
  184.1 97.8 all-gather.11
  284.5 71.5 all-gather.9
  358.5 78.4 all-gather.7
where the time goes:
time: 519 us; the launch traced here: 514 us
  waiting for transfers between devices  287 us (55%)
  blocking collectives  75.1 us (14%)
  matrix products  52.9 us (10%)
  local copies, waits for them, and re-layouts  31.6 us (6%)
  starting transfers between devices  28.1 us (5%)
  other arithmetic  24.5 us (5%)
  between operations  14.5 us (3%)
    all_gather x1, waiting for transfers between devices, body(): lax.all_gather(ref_query, 'rep', axis=0, tiled=True)  95.4 us
    all_gather x1, waiting for transfers between devices, body(): lax.all_gather(ref_key, 'rep', axis=0, tiled=True)  62.8 us
    all_to_all x1, blocking collectives, body(): lax.all_to_all(by_pack(reference_rows), 'rep', split_axis=0, concat_axis=...  55.1 us
    all_gather x1, waiting for transfers between devices, body(): lax.all_gather(ref_value, 'rep', axis=0, tiled=True)  42.2 us
    all_gather x1, waiting for transfers between devices, body(): lax.all_gather(ref_in[chosen], 'tp', axis=1, tiled=True)  41.1 us
    psum x1, blocking collectives, body(): ordered = lax.psum(partial_value, 'tp')  20 us
    dot_general x2, matrix products, attend(): jnp.einsum('pgjd,qgd->gjpq', query_four, key_three, preferred_element_typ...  19.7 us
    all_to_all x1, waiting for transfers between devices, body(): lax.all_to_all(ref_spread, 'rep', split_axis=0, concat_axis=0, tiled=True)  19.6 us
  transfers between devices with their start and end apart: 9, of which 7 were waited for; matrix products, arithmetic and copies ran while one was open for 19% of the time, Pallas kernels for 0%

commit v1 on v0

v1 whole, which is shorter than its diff:
```python
import functools

import jax
import jax.numpy as jnp
from jax import lax
from jax.experimental import pallas as pl
from jax.experimental.pallas import tpu as pltpu
from jax.sharding import PartitionSpec as P

HD = 128
NY, NZ, NX = 4, 8, 4
WIDE = 768
EPS = 1e-05
BF = jnp.bfloat16
F32 = jnp.float32


def shift_x(v, k):
    pairs = [(2 * x + c, 2 * ((x + k) % NX) + c) for x in range(NX) for c in range(2)]
    return lax.ppermute(v, "tp", pairs)


def swap_core(v):
    return lax.ppermute(v, "tp", [(t, t ^ 1) for t in range(2 * NX)])


def shift_rep(v, dy, dz):
    pairs = [
        (y * NZ + z, ((y + dy) % NY) * NZ + (z + dz) % NZ) for y in range(NY) for z in range(NZ)
    ]
    return lax.ppermute(v, "rep", pairs)


def around(v, shift):
    half = v.shape[0] // 2
    before = shift(v, 1)
    after = shift(v, -1)
    opposite_a = shift(before[:half], 1)
    opposite_b = shift(after[half:], -1)
    return v, after, opposite_a, opposite_b, before


def weights_over_rep(v):
    own, after, opp_a, opp_b, before = around(v, lambda a, k: shift_rep(a, k, 0))
    mine = jnp.stack([own, after, jnp.concatenate([opp_a, opp_b]), before])
    pieces = [(0, 0, mine)]
    low = high = mine
    for step in range(1, 4):
        low = shift_rep(low, 0, 1)
        high = shift_rep(high, 0, -1)
        pieces += [(-step, 0, low), (step, 0, high)]
    pieces += [(4, 0, shift_rep(low[:2], 0, 1)), (4, 2, shift_rep(high[2:], 0, -1))]
    return pieces


def project_kernel(plan_x, plan_keep, plan_send, n_x, n_w, k_rows, *refs):
    pos = refs[0]
    xs = refs[1 : 1 + n_x]
    ws = refs[1 + n_x : 1 + n_x + n_w]
    keep_ref, send_ref, xbuf, wbuf, sems = refs[1 + n_x + n_w :]
    copies = {"x": [], "keep": [], "send": []}
    for slot, (kind, plan, sources, dst) in enumerate(
        (
            ("x", plan_x, xs, xbuf),
            ("keep", plan_keep, ws, wbuf),
            ("send", plan_send, ws, wbuf),
        )
    ):
        for which, place in plan:
            src, at = place(pos, sources[which])
            copies[kind].append(pltpu.make_async_copy(src, dst.at[at], sems.at[slot]))
    for kind in ("x", "keep", "send"):
        for copy in copies[kind]:
            copy.start()
    rows = xbuf.shape[0]

    def wait(kind):
        for copy in copies[kind]:
            copy.wait()

    wait("x")
    squares = jnp.zeros((rows, 128), F32)

    def add_square(k, total):
        part = xbuf[:, pl.ds(pl.multiple_of(k * 128, 128), 128)].astype(F32)
        return total + part * part

    squares = lax.fori_loop(0, k_rows // 128, add_square, squares)
    keep_ref[:, WIDE:] = squares
    send_ref[:, WIDE:] = squares
    wait("keep")
    for base, out in ((0, keep_ref), (WIDE, send_ref)):
        if base:
            wait("send")

        @pl.loop(0, WIDE // 256)
        def _(n):
            src = pl.ds(pl.multiple_of(base + n * 256, 256), 256)
            dst = pl.ds(pl.multiple_of(n * 256, 256), 256)
            out[:, dst] = jnp.dot(xbuf[...], wbuf[:, src], preferred_element_type=F32)


def project(pos, xs, ws, plan_x, plan_keep, plan_send, rows, k_rows):
    hbm = pl.BlockSpec(memory_space=pl.ANY)
    vmem = pl.BlockSpec(memory_space=pltpu.VMEM)
    out = jax.ShapeDtypeStruct((rows, WIDE + 128), F32)
    return pl.pallas_call(
        functools.partial(
            project_kernel, plan_x, plan_keep, plan_send, len(xs), len(ws), k_rows
        ),
        out_shape=(out, out),
        in_specs=[pl.BlockSpec(memory_space=pltpu.SMEM)] + [hbm] * (len(xs) + len(ws)),
        out_specs=(vmem, vmem),
        scratch_shapes=[
            pltpu.VMEM((rows, k_rows), BF),
            pltpu.VMEM((k_rows, 2 * WIDE), BF),
            pltpu.SemaphoreType.DMA((3,)),
        ],
        compiler_params=pltpu.CompilerParams(vmem_limit_bytes=48 * 1024 * 1024),
        cost_estimate=pl.CostEstimate(
            flops=2 * rows * k_rows * 2 * WIDE,
            bytes_accessed=2 * k_rows * (rows + 2 * WIDE) + 8 * rows * (WIDE + 128),
            transcendentals=0,
        ),
    )(pos, *xs, *ws)


def attend_kernel(depth, keep_ref, recv_ref, seg_row, seg_col, read_ref, out_ref):
    both = keep_ref[...] + recv_ref[...]
    mean = jnp.sum(both[:, WIDE:], axis=-1, keepdims=True) * (1.0 / depth)
    rows = (both[:, :WIDE] * lax.rsqrt(mean + EPS)).astype(BF)
    tile = rows.shape[0]
    queries = jnp.concatenate([rows[:, h * HD : (h + 1) * HD] for h in range(4)], axis=0)
    keys, values = rows[:, 4 * HD : 5 * HD], rows[:, 5 * HD :]
    scores = (
        lax.dot_general(queries, keys, (((1,), (1,)), ((), ())), preferred_element_type=F32)
        * HD ** (-0.5)
    )
    ids = lax.broadcasted_iota(jnp.int32, (tile, tile), 0)
    jds = lax.broadcasted_iota(jnp.int32, (tile, tile), 1)
    allowed = (jds <= ids) & (seg_col[...] == seg_row[...])
    bias = jnp.where(allowed, 0.0, -1e30)
    bias = jnp.concatenate([bias] * 4, axis=0)
    masked = jnp.where(bias < 0.0, -1e30, scores)
    powers = jnp.exp(masked - jnp.max(masked, axis=-1, keepdims=True))
    weights = (powers / jnp.sum(powers, axis=-1, keepdims=True)).astype(BF)
    mixture = jnp.dot(weights, values, preferred_element_type=F32).astype(BF)
    total = jnp.zeros((8, tile), F32)
    for h in range(4):
        total += lax.dot_general(
            read_ref[h],
            mixture[h * tile : (h + 1) * tile],
            (((1,), (1,)), ((), ())),
            preferred_element_type=F32,
        )
    out_ref[...] = total


def attend(keep, recv, seg_row, seg_col, readout, depth):
    rows = keep.shape[0]
    tile = 128
    read = jnp.broadcast_to(readout.reshape(4, 1, HD), (4, 8, HD))
    wide = pl.BlockSpec((tile, WIDE + 128), lambda i: (i, 0))
    return pl.pallas_call(
        functools.partial(attend_kernel, depth),
        grid=(rows // tile,),
        out_shape=jax.ShapeDtypeStruct((8, rows), F32),
        in_specs=[
            wide,
            wide,
            pl.BlockSpec((1, tile), lambda i: (0, i)),
            pl.BlockSpec((tile, 1), lambda i: (i, 0)),
            pl.BlockSpec((4, 8, HD), lambda i: (0, 0, 0)),
        ],
        out_specs=pl.BlockSpec((8, tile), lambda i: (0, i)),
        cost_estimate=pl.CostEstimate(
            flops=rows * 4 * tile * HD * 4,
            bytes_accessed=rows * (WIDE + 128) * 8,
            transcendentals=rows * 4 * tile,
        ),
    )(keep, recv, seg_row, seg_col, read)


def aligned(value, step):
    return pl.multiple_of(value, step)


def x_plan(rows, width, lanes):
    plan = []
    half = rows // 2
    for which, ahead, first, count in (
        (0, 0, 0, rows),
        (1, 1, 0, rows),
        (2, 2, 0, half),
        (3, 2, half, half),
        (4, 3, 0, rows),
    ):
        for lane, size, offset in lanes:

            def place(pos, src, ahead=ahead, first=first, count=count, lane=lane, size=size, offset=offset):
                origin = lax.rem(pos[0] + ahead, NX)
                at = aligned(origin * width + offset(pos[1]), 128)
                return src.at[:, pl.ds(lane, size)], (pl.ds(first, count), pl.ds(at, size))

            plan.append((which, place))
    return plan


def body(
    reference_rows,
    critic_rows,
    segment_ids,
    pack_dest,
    ref_query,
    ref_key,
    ref_value,
    critic_query,
    critic_key,
    critic_value,
    ref_readout,
    critic_readout,
):
    del pack_dest
    rep, tp = lax.axis_index("rep"), lax.axis_index("tp")
    x, core = tp // 2, tp % 2
    y, z = rep // NZ, rep % NZ
    pos = jnp.stack([x, core, y, z]).astype(jnp.int32)
    first = core == 0

    ref_w = jnp.concatenate([ref_query, ref_key, ref_value], axis=1)
    upper, lower = ref_w[:128], ref_w[128:]
    ref_keep = jnp.where(first, upper, lower)
    ref_send = swap_core(jnp.where(first, lower, upper))
    keep_all = lax.all_gather(ref_keep, "rep", axis=0, tiled=True)
    send_pieces = weights_over_rep(ref_send)

    critic_w = [w.reshape(NX, 2, 512, -1) for w in (critic_query, critic_key, critic_value)]
    critic_send = swap_core(
        jnp.concatenate(
            [lax.dynamic_index_in_dim(w, 1 - core, 1, keepdims=False) for w in critic_w], axis=-1
        )
    )

    critic_shards = around(critic_rows, shift_x)

    low = jnp.concatenate([reference_rows[:, k : k + 128] for k in range(0, 1024, 256)], axis=1)
    high = jnp.concatenate([reference_rows[:, k : k + 128] for k in range(128, 1024, 256)], axis=1)
    ref_mine = jnp.where(first, low, high)
    ref_other = swap_core(jnp.where(first, high, low))
    ref_rows = jnp.concatenate([ref_mine, ref_other], axis=1)

    chunk = 512
    ref_shards = [
        around(ref_rows[start : start + chunk], shift_x) for start in range(0, 1024, chunk)
    ]

    seg_row = segment_ids.reshape(1, -1)
    seg_col = segment_ids.reshape(-1, 1)

    def critic_keep_place(lane, size):
        def make(k):
            def place(pos, src):
                return (
                    src.at[pl.ds(aligned((2 * k + pos[1]) * 512, 512), 512), :],
                    (pl.ds(k * 512, 512), pl.ds(lane, size)),
                )

            return place

        return [make(k) for k in range(NX)]

    plan_keep = [
        (i, place)
        for i, (lane, size) in enumerate(((0, 512), (512, 128), (640, 128)))
        for place in critic_keep_place(lane, size)
    ]

    def critic_send_place(k):
        def place(pos, src):
            return src.at[k], (pl.ds(k * 512, 512), pl.ds(WIDE, WIDE))

        return place

    plan_send = [(3, critic_send_place(k)) for k in range(NX)]
    keep, send = project(
        pos,
        list(critic_shards),
        [critic_query, critic_key, critic_value, critic_send],
        x_plan(1024, 512, [(0, 512, lambda c: 0)]),
        plan_keep,
        plan_send,
        1024,
        2048,
    )
    critic_part = attend(keep, swap_core(send), seg_row, seg_col, critic_readout, 4096)[:1]

    def ref_keep_place(k):
        def place(pos, src):
            return src.at[pl.ds(k * 1024, 1024), :], (pl.ds(k * 1024, 1024), pl.ds(0, WIDE))

        return place

    plan_keep = [(0, ref_keep_place(k)) for k in range(NX)]
    plan_send = []
    for index, (dz, dy0, piece) in enumerate(send_pieces):
        for j in range(piece.shape[0]):

            def place(pos, src, dz=dz, dy=dy0 + j, j=j):
                origin = lax.rem(pos[2] + dy, NY) * NZ + lax.rem(pos[3] + dz + NZ, NZ)
                return src.at[j], (pl.ds(aligned(origin * 128, 128), 128), pl.ds(WIDE, WIDE))

            plan_send.append((1 + index, place))
    ref_ws = [keep_all] + [piece for _, _, piece in send_pieces]
    lanes = [(0, 512, lambda c: c * 512), (512, 512, lambda c: (1 - c) * 512)]
    ref_parts = []
    for index, shards in enumerate(ref_shards):
        start = index * chunk
        keep, send = project(
            pos,
            list(shards),
            ref_ws,
            x_plan(chunk, 1024, lanes),
            plan_keep,
            plan_send,
            chunk,
            4096,
        )
        ref_parts.append(
            attend(
                keep,
                swap_core(send),
                seg_row[:, start : start + chunk],
                seg_col[start : start + chunk],
                ref_readout,
                8192,
            )[:1]
        )
    partial = jnp.concatenate([jnp.concatenate(ref_parts, axis=1), critic_part], axis=0)
    scores = lax.psum(partial, "tp")
    scores = jnp.where(seg_row >= 0, scores, 0.0)
    return scores[0], scores[1]


def solution(mesh):
    return jax.shard_map(
        body,
        mesh=mesh,
        in_specs=(
            P("rep", "tp"),
            P("rep", "tp"),
            P("rep"),
            P("rep", None),
            P("rep", "tp"),
            P("rep", "tp"),
            P("rep", "tp"),
            P(None, "tp"),
            P(None, "tp"),
            P(None, "tp"),
            P("tp"),
            P("tp"),
        ),
        out_specs=(P("rep"), P("rep")),
        check_vma=False,
    )
```

time: 519 us -> 239 us (0.46)
  waiting for transfers between devices: 287 us -> 66.6 us
  Pallas kernels: 0 us -> 62.7 us
  blocking collectives: 75.1 us -> 12.5 us
  matrix products: 52.9 us -> 0 us
  other arithmetic: 24.5 us -> 5.29 us
  starting transfers between devices: 28.1 us -> 41.3 us
    all_gather x5 -> x1, waiting for transfers between devices: 241 us -> 0.01 us  [body(): keep_all = lax.all_gather(ref_keep, 'rep', axis=0, tiled=True)]
    ppermute x0 -> x30, waiting for transfers between devices: none -> 66.6 us  [the longest x12 47.6 us: shift_rep(): return lax.ppermute(v, 'rep', pairs)]
    pallas_call x0 -> x6, Pallas kernels: none -> 62.7 us  [the longest x3 41.9 us: project(): pl.pallas_call(functools.partial(project_kernel, plan_x, plan_keep, plan_...]
    all_to_all x1 -> x0, blocking collectives: 55.1 us -> none  [body(): lax.all_to_all(by_pack(reference_rows), 'rep', split_axis=0, concat_axis=...]
    dot_general x8 -> x0, matrix products: 52.9 us -> none  [the longest x2 19.7 us: attend(): jnp.einsum('pgjd,qgd->gjpq', query_four, key_three, preferred_element_typ...]
    all_to_all x4 -> x0, waiting for transfers between devices: 43.9 us -> none  [the longest x1 19.6 us: body(): lax.all_to_all(ref_spread, 'rep', split_axis=0, concat_axis=0, tiled=True)]
    ppermute x0 -> x30, starting transfers between devices: none -> 41.3 us  [the longest x12 17.1 us: shift_rep(): return lax.ppermute(v, 'rep', pairs)]
    all_to_all x4 -> x0, starting transfers between devices: 27.9 us -> none  [the longest x1 12 us: body(): lax.all_to_all(by_pack(segment_ids), 'rep', split_axis=0, concat_axis=0,...]
  transfers between devices with their start and end apart: 9 -> 31, of which waited for: 7 -> 10; matrix products, arithmetic and copies ran while one was open for 19% -> 8% of each run, Pallas kernels for 0% -> 24%
where the time goes in v1:
time: 239 us; the launch traced here: 238 us
  waiting for transfers between devices  66.6 us (28%)
  Pallas kernels  62.7 us (26%)
  starting transfers between devices  41.3 us (17%)
  local copies, waits for them, and re-layouts  34.9 us (15%)
  between operations  14.5 us (6%)
  blocking collectives  12.5 us (5%)
  other arithmetic  5.29 us (2%)
    ppermute x12, waiting for transfers between devices, shift_rep(): return lax.ppermute(v, 'rep', pairs)  47.6 us
    pallas_call x3, Pallas kernels, project(): pl.pallas_call(functools.partial(project_kernel, plan_x, plan_keep, plan_...  41.9 us
    pallas_call x3, Pallas kernels, attend(): pl.pallas_call(functools.partial(attend_kernel, depth), grid=(rows // til...  20.8 us
    unnamed x60, local copies, waits for them, and re-layouts  18.7 us
    ppermute x12, starting transfers between devices, shift_rep(): return lax.ppermute(v, 'rep', pairs)  17.1 us
    ppermute x12, waiting for transfers between devices, shift_x(): return lax.ppermute(v, 'tp', pairs)  15.8 us
    ppermute x12, starting transfers between devices, shift_x(): return lax.ppermute(v, 'tp', pairs)  12.6 us
    psum x1, blocking collectives, body(): scores = lax.psum(partial, 'tp')  12.5 us
  transfers between devices with their start and end apart: 31, of which 10 were waited for; matrix products, arithmetic and copies ran while one was open for 8% of the time, Pallas kernels for 24%

profile of v1, /device:TPU:1, one launch (start us, length us, event | category | flops | bytes accessed | tf_op | source)
XLA Modules:
  0.0 237.7 jit_solution(8153447730764943320)
XLA Ops:
  7.2 1.0 constant_dynamic-update-slice_fusion.2
  10.8 1.1 dynamic-slice_bitcast_fusion.1
  11.9 1.7 dynamic-slice_bitcast_fusion
  13.7 2.0 pad_maximum_fusion
  15.6 3.2 %collective-permute-start.28 = (bf16[4,512,768]{2,1,0:T(8,128)(2,1)}, bf16[4,512,768]{2,1,0:T(8,128)(2,1)}, u32[]{:S(2)}, u32[]{:S(2)}) collective-permute-start(bf16[4,512,768]{2,1,0:T(8,128)(2,1)} %pad_maximum_fusion), channel_id=1, source_target_pairs={{0,1},{1,0},{2,3},{3,2},{4,5},{5,4},{6,7},{7,6},{8,9},{9,8},{10,11... | collective-permute-start | bytes 9437192 | tf_op jit(solution)/shard_map/ppermute | solution.py:24
  20.0 1.1 collective-permute-start
  21.2 3.1 %collective-permute-done.5 = bf16[128,768]{1,0:T(8,128)(2,1)S(1)} collective-permute-done((bf16[128,768]{1,0:T(8,128)(2,1)S(1)}, bf16[128,768]{1,0:T(8,128)(2,1)S(1)}, u32[]{:S(2)}, u32[]{:S(2)}) %collective-permute-start.5) | collective-permute-done | bytes 196640 | tf_op jit(solution)/shard_map/ppermute | solution.py:24
  24.3 2.7 %collective-permute-start.6 = (bf16[128,768]{1,0:T(8,128)(2,1)S(1)}, bf16[128,768]{1,0:T(8,128)(2,1)S(1)}, u32[]{:S(2)}, u32[]{:S(2)}) collective-permute-start(bf16[128,768]{1,0:T(8,128)(2,1)S(1)} %collective-permute-done.5), channel_id=1, source_target_pairs={{0,192},{8,200},{16,208},{24,216},{32,224},{40,232},{48,240},{56,2... | collective-permute-start | bytes 589832 | tf_op jit(solution)/shard_map/ppermute | solution.py:31
  27.0 5.4 %collective-permute-done.7 = bf16[128,768]{1,0:T(8,128)(2,1)S(1)} collective-permute-done((bf16[128,768]{1,0:T(8,128)(2,1)S(1)}, bf16[128,768]{1,0:T(8,128)(2,1)S(1)}, u32[]{:S(2)}, u32[]{:S(2)}) %collective-permute-start.7) | collective-permute-done | bytes 196640 | tf_op jit(solution)/shard_map/ppermute | solution.py:31
  32.9 5.7 %collective-permute-done.8 = bf16[64,768]{1,0:T(8,128)(2,1)S(1)} collective-permute-done((bf16[64,768]{1,0:T(8,128)(2,1)S(1)}, bf16[64,768]{1,0:T(8,128)(2,1)S(1)}, u32[]{:S(2)}, u32[]{:S(2)}) %collective-permute-start.8) | collective-permute-done | bytes 98336 | tf_op jit(solution)/shard_map/ppermute | solution.py:31
  39.5 3.0 %collective-permute-done.9 = bf16[64,768]{1,0:T(8,128)(2,1)S(1)} collective-permute-done((bf16[64,768]{1,0:T(8,128)(2,1)S(1)}, bf16[64,768]{1,0:T(8,128)(2,1)S(1)}, u32[]{:S(2)}, u32[]{:S(2)}) %collective-permute-start.9) | collective-permute-done | bytes 98336 | tf_op jit(solution)/shard_map/ppermute | solution.py:31
  44.4 4.4 %collective-permute-start.11 = (bf16[4,128,768]{2,1,0:T(8,128)(2,1)S(1)}, bf16[4,128,768]{2,1,0:T(8,128)(2,1)S(1)}, u32[]{:S(2)}, u32[]{:S(2)}) collective-permute-start(bf16[4,128,768]{2,1,0:T(8,128)(2,1)S(1)} %pad_maximum_fusion.4.refs_7_), channel_id=1, source_target_pairs={{0,56},{8,0},{16,8},{24,16},{32,24},{40,32},{48,40},{56,48},{64,12... | collective-permute-start | bytes 2359304 | tf_op jit(solution)/shard_map/ppermute | solution.py:31
  48.9 1.7 fusion
  50.6 4.9 %collective-permute-done.24.refs_2_ = bf16[1024,512]{1,0:T(8,128)(2,1)S(1)} collective-permute-done((bf16[1024,512]{1,0:T(8,128)(2,1)S(1)}, bf16[1024,512]{1,0:T(8,128)(2,1)S(1)}, u32[]{:S(2)}, u32[]{:S(2)}) %collective-permute-start.24) | collective-permute-done | bytes 1048608 | tf_op jit(solution)/shard_map/ppermute | solution.py:20
  55.6 10.3 %collective-permute-done.10.refs_8_ = bf16[4,128,768]{2,1,0:T(8,128)(2,1)S(1)} collective-permute-done((bf16[4,128,768]{2,1,0:T(8,128)(2,1)S(1)}, bf16[4,128,768]{2,1,0:T(8,128)(2,1)S(1)}, u32[]{:S(2)}, u32[]{:S(2)}) %collective-permute-start.10) | collective-permute-done | bytes 786464 | tf_op jit(solution)/shard_map/ppermute | solution.py:31
  65.9 1.7 collective-permute-start.27
  68.5 2.7 %collective-permute-start.13 = (bf16[4,128,768]{2,1,0:T(8,128)(2,1)S(1)}, bf16[4,128,768]{2,1,0:T(8,128)(2,1)S(1)}, u32[]{:S(2)}, u32[]{:S(2)}) collective-permute-start(bf16[4,128,768]{2,1,0:T(8,128)(2,1)S(1)} %collective-permute-done.11.refs_9_), channel_id=1, source_target_pairs={{0,56},{8,0},{16,8},{24,16},{32,24},{40,32},{48,40},{56,48},{64,12... | collective-permute-start | bytes 2359304 | tf_op jit(solution)/shard_map/ppermute | solution.py:31
  72.1 4.6 %collective-permute-done.27.refs_4_ = bf16[512,512]{1,0:T(8,128)(2,1)S(1)} collective-permute-done((bf16[512,512]{1,0:T(8,128)(2,1)S(1)}, bf16[512,512]{1,0:T(8,128)(2,1)S(1)}, u32[]{:S(2)}, u32[]{:S(2)}) %collective-permute-start.27) | collective-permute-done | bytes 524320 | tf_op jit(solution)/shard_map/ppermute | solution.py:20
  77.5 3.2 %collective-permute-start.1 = (bf16[512,1024]{1,0:T(8,128)(2,1)}, bf16[512,1024]{1,0:T(8,128)(2,1)}, u32[]{:S(2)}, u32[]{:S(2)}) collective-permute-start(bf16[512,1024]{1,0:T(8,128)(2,1)} %get-tuple-element.14.refs_1_), channel_id=1, source_target_pairs={{0,6},{1,7},{2,0},{3,1},{4,2},{5,3},{6,4},{7,5},{8,14},{9,15},{10,... | collective-permute-start | bytes 3145736 | tf_op jit(solution)/shard_map/ppermute | solution.py:20
  80.7 23.2 %collective-permute-done.12.refs_10_ = bf16[4,128,768]{2,1,0:T(8,128)(2,1)S(1)} collective-permute-done((bf16[4,128,768]{2,1,0:T(8,128)(2,1)S(1)}, bf16[4,128,768]{2,1,0:T(8,128)(2,1)S(1)}, u32[]{:S(2)}, u32[]{:S(2)}) %collective-permute-start.12) | collective-permute-done | bytes 786464 | tf_op jit(solution)/shard_map/ppermute | solution.py:31
  105.6 1.8 collective-permute-start.19
  107.4 2.7 %collective-permute-start.15 = (bf16[4,128,768]{2,1,0:T(8,128)(2,1)}, bf16[4,128,768]{2,1,0:T(8,128)(2,1)S(1)}, u32[]{:S(2)}, u32[]{:S(2)}) collective-permute-start(bf16[4,128,768]{2,1,0:T(8,128)(2,1)} %copy-done.11), channel_id=1, source_target_pairs={{0,56},{8,0},{16,8},{24,16},{32,24},{40,32},{48,40},{56,48},{64,12... | collective-permute-start | bytes 2359304 | tf_op jit(solution)/shard_map/ppermute | solution.py:31
  110.2 1.2 copy-done.2
  111.4 1.2 copy-done.4
  112.7 1.0 copy-done.14
  113.7 13.7 %shard_map.126 = (f32[1024,896]{1,0:T(8,128)}, f32[1024,896]{1,0:T(8,128)}) custom-call(s32[4]{0:T(128)S(1)} %pad_add_fusion.refs_0_, bf16[1024,512]{1,0:T(8,128)(2,1)S(1)} %copy-done.4, bf16[1024,512]{1,0:T(8,128)(2,1)S(1)} %copy-done.2, bf16[512,512]{1,0:T(8,128)(2,1)S(1)} %collective-permute-done.26.refs_3_, bf16[512,512]{1,0:T(8,128)(2,1)S(1)} %copy-done.14, ...), custom_call_target="tpu_custom_call" | custom-call | flops 6442450944 | bytes 17825792 | tf_op jit(solution)/shard_map/pallas_call | solution.py:107
  127.5 5.7 %collective-permute-start.29 = (f32[1024,896]{1,0:T(8,128)}, f32[1024,896]{1,0:T(8,128)}, u32[]{:S(2)}, u32[]{:S(2)}) collective-permute-start(f32[1024,896]{1,0:T(8,128)} %get-tuple-element.13), channel_id=1, source_target_pairs={{0,1},{1,0},{2,3},{3,2},{4,5},{5,4},{6,7},{7,6},{8,9},{9,8},{10,11... | collective-permute-start | bytes 11010056 | tf_op jit(solution)/shard_map/ppermute | solution.py:24
  133.2 1.1 slice.134
  134.2 1.1 slice.135
  135.5 2.6 %collective-permute-start.4 = (bf16[256,1024]{1,0:T(8,128)(2,1)S(1)}, bf16[256,1024]{1,0:T(8,128)(2,1)S(1)}, u32[]{:S(2)}, u32[]{:S(2)}) collective-permute-start(bf16[256,1024]{1,0:T(8,128)(2,1)S(1)} %slice.135), channel_id=1, source_target_pairs={{0,6},{1,7},{2,0},{3,1},{4,2},{5,3},{6,4},{7,5},{8,14},{9,15},{10,... | collective-permute-start | bytes 1572872 | tf_op jit(solution)/shard_map/ppermute | solution.py:20
  138.3 2.7 %collective-permute-start.17 = (bf16[2,128,768]{2,1,0:T(8,128)(2,1)S(1)}, bf16[2,128,768]{2,1,0:T(8,128)(2,1)S(1)}, u32[]{:S(2)}, u32[]{:S(2)}) collective-permute-start(bf16[2,128,768]{2,1,0:T(8,128)(2,1)S(1)} %slice.141), channel_id=1, source_target_pairs={{0,56},{8,0},{16,8},{24,16},{32,24},{40,32},{48,40},{56,48},{64,12... | collective-permute-start | bytes 1179656 | tf_op jit(solution)/shard_map/ppermute | solution.py:31
  140.9 1.9 slice.144
  142.9 1.9 slice.145
  144.8 5.4 %collective-permute-done.3.refs_3_ = bf16[256,1024]{1,0:T(8,128)(2,1)S(1)} collective-permute-done((bf16[256,1024]{1,0:T(8,128)(2,1)S(1)}, bf16[256,1024]{1,0:T(8,128)(2,1)S(1)}, u32[]{:S(2)}, u32[]{:S(2)}) %collective-permute-start.3) | collective-permute-done | bytes 524320 | tf_op jit(solution)/shard_map/ppermute | solution.py:20
  151.0 2.7 %collective-permute-start.22 = (bf16[256,1024]{1,0:T(8,128)(2,1)}, bf16[256,1024]{1,0:T(8,128)(2,1)}, u32[]{:S(2)}, u32[]{:S(2)}) collective-permute-start(bf16[256,1024]{1,0:T(8,128)(2,1)} %slice.145), channel_id=1, source_target_pairs={{0,6},{1,7},{2,0},{3,1},{4,2},{5,3},{6,4},{7,5},{8,14},{9,15},{10,... | collective-permute-start | bytes 1572872 | tf_op jit(solution)/shard_map/ppermute | solution.py:20
  155.3 1.1 copy-done.10
  156.4 1.1 copy-done.12
  157.5 1.0 copy-done.16
  158.6 1.0 copy-done.18
  160.6 13.9 %shard_map.122 = (f32[512,896]{1,0:T(8,128)}, f32[512,896]{1,0:T(8,128)}) custom-call(s32[4]{0:T(128)S(1)} %pad_add_fusion.refs_0_, bf16[512,1024]{1,0:T(8,128)(2,1)} %get-tuple-element.14.refs_1_, bf16[512,1024]{1,0:T(8,128)(2,1)} %collective-permute-done.1.refs_2_, bf16[256,1024]{1,0:T(8,128)(2,1)S(1)} %collective-permute-done.3.refs_3_, ...), custom_call_target="tpu_custom_call" | custom-call | flops 6442450944 | bytes 20447232 | tf_op jit(solution)/shard_map/pallas_call | solution.py:107
  174.5 1.4 collective-permute-start.18
  176.0 14.2 %shard_map.124 = (f32[512,896]{1,0:T(8,128)}, f32[512,896]{1,0:T(8,128)}) custom-call(s32[4]{0:T(128)S(1)} %pad_add_fusion.refs_0_, bf16[512,1024]{1,0:T(8,128)(2,1)} %get-tuple-element.15.refs_1_, bf16[512,1024]{1,0:T(8,128)(2,1)} %collective-permute-done.19.refs_2_, bf16[256,1024]{1,0:T(8,128)(2,1)} %collective-permute-done.21.refs_3_, ...), custom_call_target="tpu_custom_call" | custom-call | flops 6442450944 | bytes 20447232 | tf_op jit(solution)/shard_map/pallas_call | solution.py:107
  192.1 1.1 copy.21.seg_col
  194.3 9.7 %shard_map.127 = f32[8,1024]{1,0:T(8,128)} custom-call(f32[1024,896]{1,0:T(8,128)} %get-tuple-element.12.keep_ref, f32[1024,896]{1,0:T(8,128)} %collective-permute-done.29.recv_ref, s32[1,1024]{1,0:T(1,128)} %bitcast.38, s32[1024,1]{1,0:T(8,128)} %copy.21.seg_col, bf16[4,8,128]{2,1,0:T(8,128)(2,1)} %broadcast_in_dim.33.read_ref), custom_call_target="tpu_custom_call" | custom-call | flops 268435456 | bytes 7340032 | tf_op jit(solution)/shard_map/pallas_call | solution.py:164
  204.6 5.6 %shard_map.123 = f32[8,512]{1,0:T(8,128)} custom-call(f32[512,896]{1,0:T(8,128)} %get-tuple-element.8.keep_ref, f32[512,896]{1,0:T(8,128)} %collective-permute-done.18.recv_ref, s32[1,512]{1,0:T(1,128)} %get-tuple-element.32.seg_row, s32[512,1]{1,0:T(8,128)} %copy.16.seg_col, bf16[4,8,128]{2,1,0:T(8,128)(2,1)} %broadcast_in_dim.31.read_ref), custom_call_target="tpu_custom_call" | custom-call | flops 134217728 | bytes 3670016 | tf_op jit(solution)/shard_map/pallas_call | solution.py:164
  210.2 1.3 copy-done.23
  211.5 5.6 %shard_map.125 = f32[8,512]{1,0:T(8,128)} custom-call(f32[512,896]{1,0:T(8,128)} %get-tuple-element.10.keep_ref, f32[512,896]{1,0:T(8,128)} %copy-done.23, s32[1,512]{1,0:T(1,128)} %get-tuple-element.33.seg_row, s32[512,1]{1,0:T(8,128)} %copy.17.seg_col, bf16[4,8,128]{2,1,0:T(8,128)(2,1)} %broadcast_in_dim.31.read_ref), custom_call_target="tpu_custom_call" | custom-call | flops 134217728 | bytes 3670016 | tf_op jit(solution)/shard_map/pallas_call | solution.py:164
  217.8 12.5 %psum.7 = f32[2,1024]{1,0:T(2,128)S(1)} all-reduce(f32[2,1024]{1,0:T(2,128)S(1)} %pad_maximum_fusion.5), channel_id=1, replica_groups=mesh['rep'=32,'tp'=8] {'tp'}, use_global_device_ids=true, to_apply=%region_0.1 | all-reduce | flops 2048 | bytes 16384 | tf_op jit(solution)/shard_map/psum | solution.py:339
  (119 shorter events, 20.1 us)
Async XLA Ops:
  7.2 3.6 %copy-start = (bf16[4096,128]{1,0:T(8,128)(2,1)S(1)}, bf16[4096,128]{1,0:T(8,128)(2,1)}, u32[]{:S(2)}) copy-start(bf16[4096,128]{1,0:T(8,128)(2,1)} %refs_7_.1) | copy-start | bytes 3145732
  7.2 148.1 %all-gather.2.cloned.1.call-start = ((), (), s32[]{:S(2)}) async-start(), calls=%async_computation | async-start | bytes 6488064 | tf_op jit(solution)/shard_map/all_gather | solution.py:234
  13.6 5.2 %copy-start.3 = (bf16[1024,512]{1,0:T(8,128)(2,1)S(1)}, bf16[1024,512]{1,0:T(8,128)(2,1)}, u32[]{:S(2)}) copy-start(bf16[1024,512]{1,0:T(8,128)(2,1)} %refs_1_.1) | copy-start | bytes 3145732
  13.6 5.2 %copy-start.22 = (bf16[1024,1024]{1,0:T(8,128)(2,1)S(1)}, bf16[1024,1024]{1,0:T(8,128)(2,1)}, u32[]{:S(2)}) copy-start(bf16[1024,1024]{1,0:T(8,128)(2,1)} %param.12) | copy-start | bytes 6291460
  15.6 91.8 %collective-permute-start.28 = (bf16[4,512,768]{2,1,0:T(8,128)(2,1)}, bf16[4,512,768]{2,1,0:T(8,128)(2,1)}, u32[]{:S(2)}, u32[]{:S(2)}) collective-permute-start(bf16[4,512,768]{2,1,0:T(8,128)(2,1)} %pad_maximum_fusion), channel_id=1, source_target_pairs={{0,1},{1,0},{2,3},{3,2},{4,5},{5,4},{6,7},{7,6},{8,9},{9,8},{10,11... | collective-permute-start | bytes 9437192 | tf_op jit(solution)/shard_map/ppermute | solution.py:24
  18.9 5.4 %collective-permute-start.5 = (bf16[128,768]{1,0:T(8,128)(2,1)S(1)}, bf16[128,768]{1,0:T(8,128)(2,1)S(1)}, u32[]{:S(2)}, u32[]{:S(2)}) collective-permute-start(bf16[128,768]{1,0:T(8,128)(2,1)S(1)} %get-tuple-element.26), channel_id=1, source_target_pairs={{0,1},{1,0},{2,3},{3,2},{4,5},{5,4},{6,7},{7,6},{8,9},{9,8},{10,11... | collective-permute-start | bytes 589832 | tf_op jit(solution)/shard_map/ppermute | solution.py:24
  18.9 25.5 %collective-permute-start.25 = (bf16[1024,512]{1,0:T(8,128)(2,1)S(1)}, bf16[1024,512]{1,0:T(8,128)(2,1)S(1)}, u32[]{:S(2)}, u32[]{:S(2)}) collective-permute-start(bf16[1024,512]{1,0:T(8,128)(2,1)S(1)} %copy-done.3), channel_id=1, source_target_pairs={{0,2},{1,3},{2,4},{3,5},{4,6},{5,7},{6,0},{7,1},{8,10},{9,11},{10,... | collective-permute-start | bytes 3145736 | tf_op jit(solution)/shard_map/ppermute | solution.py:20
  20.0 28.8 %collective-permute-start = (bf16[1024,512]{1,0:T(8,128)(2,1)S(1)}, bf16[1024,512]{1,0:T(8,128)(2,1)S(1)}, u32[]{:S(2)}, u32[]{:S(2)}) collective-permute-start(bf16[1024,512]{1,0:T(8,128)(2,1)S(1)} %get-tuple-element.17), channel_id=1, source_target_pairs={{0,1},{1,0},{2,3},{3,2},{4,5},{5,4},{6,7},{7,6},{8,9},{9,8},{10,11... | collective-permute-start | bytes 3145736 | tf_op jit(solution)/shard_map/ppermute | solution.py:24
  24.3 8.0 %collective-permute-start.7 = (bf16[128,768]{1,0:T(8,128)(2,1)S(1)}, bf16[128,768]{1,0:T(8,128)(2,1)S(1)}, u32[]{:S(2)}, u32[]{:S(2)}) collective-permute-start(bf16[128,768]{1,0:T(8,128)(2,1)S(1)} %collective-permute-done.5), channel_id=1, source_target_pairs={{0,64},{8,72},{16,80},{24,88},{32,96},{40,104},{48,112},{56,120},{... | collective-permute-start | bytes 589832 | tf_op jit(solution)/shard_map/ppermute | solution.py:31
  24.3 8.5 %collective-permute-start.6 = (bf16[128,768]{1,0:T(8,128)(2,1)S(1)}, bf16[128,768]{1,0:T(8,128)(2,1)S(1)}, u32[]{:S(2)}, u32[]{:S(2)}) collective-permute-start(bf16[128,768]{1,0:T(8,128)(2,1)S(1)} %collective-permute-done.5), channel_id=1, source_target_pairs={{0,192},{8,200},{16,208},{24,216},{32,224},{40,232},{48,240},{56,2... | collective-permute-start | bytes 589832 | tf_op jit(solution)/shard_map/ppermute | solution.py:31
  32.3 23.2 %collective-permute-start.24 = (bf16[1024,512]{1,0:T(8,128)(2,1)S(1)}, bf16[1024,512]{1,0:T(8,128)(2,1)S(1)}, u32[]{:S(2)}, u32[]{:S(2)}) collective-permute-start(bf16[1024,512]{1,0:T(8,128)(2,1)S(1)} %copy-done.3), channel_id=1, source_target_pairs={{0,6},{1,7},{2,0},{3,1},{4,2},{5,3},{6,4},{7,5},{8,14},{9,15},{10,... | collective-permute-start | bytes 3145736 | tf_op jit(solution)/shard_map/ppermute | solution.py:20
  32.8 5.9 %collective-permute-start.8 = (bf16[64,768]{1,0:T(8,128)(2,1)S(1)}, bf16[64,768]{1,0:T(8,128)(2,1)S(1)}, u32[]{:S(2)}, u32[]{:S(2)}) collective-permute-start(bf16[64,768]{1,0:T(8,128)(2,1)S(1)} %slice.138), channel_id=1, source_target_pairs={{0,64},{8,72},{16,80},{24,88},{32,96},{40,104},{48,112},{56,120},{... | collective-permute-start | bytes 294920 | tf_op jit(solution)/shard_map/ppermute | solution.py:31
  38.6 4.0 %collective-permute-start.9 = (bf16[64,768]{1,0:T(8,128)(2,1)S(1)}, bf16[64,768]{1,0:T(8,128)(2,1)S(1)}, u32[]{:S(2)}, u32[]{:S(2)}) collective-permute-start(bf16[64,768]{1,0:T(8,128)(2,1)S(1)} %slice.139), channel_id=1, source_target_pairs={{0,192},{8,200},{16,208},{24,216},{32,224},{40,232},{48,240},{56,2... | collective-permute-start | bytes 294920 | tf_op jit(solution)/shard_map/ppermute | solution.py:31
  42.7 23.2 %collective-permute-start.10 = (bf16[4,128,768]{2,1,0:T(8,128)(2,1)S(1)}, bf16[4,128,768]{2,1,0:T(8,128)(2,1)S(1)}, u32[]{:S(2)}, u32[]{:S(2)}) collective-permute-start(bf16[4,128,768]{2,1,0:T(8,128)(2,1)S(1)} %pad_maximum_fusion.4.refs_7_), channel_id=1, source_target_pairs={{0,8},{8,16},{16,24},{24,32},{32,40},{40,48},{48,56},{56,0},{64,72... | collective-permute-start | bytes 2359304 | tf_op jit(solution)/shard_map/ppermute | solution.py:31
  44.4 23.2 %collective-permute-start.11 = (bf16[4,128,768]{2,1,0:T(8,128)(2,1)S(1)}, bf16[4,128,768]{2,1,0:T(8,128)(2,1)S(1)}, u32[]{:S(2)}, u32[]{:S(2)}) collective-permute-start(bf16[4,128,768]{2,1,0:T(8,128)(2,1)S(1)} %pad_maximum_fusion.4.refs_7_), channel_id=1, source_target_pairs={{0,56},{8,0},{16,8},{24,16},{32,24},{40,32},{48,40},{56,48},{64,12... | collective-permute-start | bytes 2359304 | tf_op jit(solution)/shard_map/ppermute | solution.py:31
  48.8 19.7 %collective-permute-start.26 = (bf16[512,512]{1,0:T(8,128)(2,1)S(1)}, bf16[512,512]{1,0:T(8,128)(2,1)S(1)}, u32[]{:S(2)}, u32[]{:S(2)}) collective-permute-start(bf16[512,512]{1,0:T(8,128)(2,1)S(1)} %slice.148), channel_id=1, source_target_pairs={{0,2},{1,3},{2,4},{3,5},{4,6},{5,7},{6,0},{7,1},{8,10},{9,11},{10,... | collective-permute-start | bytes 1572872 | tf_op jit(solution)/shard_map/ppermute | solution.py:20
  55.5 12.1 %copy-start.1 = (bf16[1024,512]{1,0:T(8,128)(2,1)}, bf16[1024,512]{1,0:T(8,128)(2,1)S(1)}, u32[]{:S(2)}) copy-start(bf16[1024,512]{1,0:T(8,128)(2,1)S(1)} %collective-permute-done.24.refs_2_) | copy-start | bytes 3145732
  55.6 51.9 %collective-permute-start.2 = (bf16[512,1024]{1,0:T(8,128)(2,1)}, bf16[512,1024]{1,0:T(8,128)(2,1)}, u32[]{:S(2)}, u32[]{:S(2)}) collective-permute-start(bf16[512,1024]{1,0:T(8,128)(2,1)} %get-tuple-element.14.refs_1_), channel_id=1, source_target_pairs={{0,2},{1,3},{2,4},{3,5},{4,6},{5,7},{6,0},{7,1},{8,10},{9,11},{10,... | collective-permute-start | bytes 3145736 | tf_op jit(solution)/shard_map/ppermute | solution.py:20
  65.9 10.8 %collective-permute-start.27 = (bf16[512,512]{1,0:T(8,128)(2,1)S(1)}, bf16[512,512]{1,0:T(8,128)(2,1)S(1)}, u32[]{:S(2)}, u32[]{:S(2)}) collective-permute-start(bf16[512,512]{1,0:T(8,128)(2,1)S(1)} %slice.149), channel_id=1, source_target_pairs={{0,6},{1,7},{2,0},{3,1},{4,2},{5,3},{6,4},{7,5},{8,14},{9,15},{10,... | collective-permute-start | bytes 1572872 | tf_op jit(solution)/shard_map/ppermute | solution.py:20
  67.6 36.2 %collective-permute-start.12 = (bf16[4,128,768]{2,1,0:T(8,128)(2,1)S(1)}, bf16[4,128,768]{2,1,0:T(8,128)(2,1)S(1)}, u32[]{:S(2)}, u32[]{:S(2)}) collective-permute-start(bf16[4,128,768]{2,1,0:T(8,128)(2,1)S(1)} %collective-permute-done.10.refs_8_), channel_id=1, source_target_pairs={{0,8},{8,16},{16,24},{24,32},{32,40},{40,48},{48,56},{56,0},{64,72... | collective-permute-start | bytes 2359304 | tf_op jit(solution)/shard_map/ppermute | solution.py:31
  68.5 35.3 %collective-permute-start.13 = (bf16[4,128,768]{2,1,0:T(8,128)(2,1)S(1)}, bf16[4,128,768]{2,1,0:T(8,128)(2,1)S(1)}, u32[]{:S(2)}, u32[]{:S(2)}) collective-permute-start(bf16[4,128,768]{2,1,0:T(8,128)(2,1)S(1)} %collective-permute-done.11.refs_9_), channel_id=1, source_target_pairs={{0,56},{8,0},{16,8},{24,16},{32,24},{40,32},{48,40},{56,48},{64,12... | collective-permute-start | bytes 2359304 | tf_op jit(solution)/shard_map/ppermute | solution.py:31
  77.5 49.9 %collective-permute-start.1 = (bf16[512,1024]{1,0:T(8,128)(2,1)}, bf16[512,1024]{1,0:T(8,128)(2,1)}, u32[]{:S(2)}, u32[]{:S(2)}) collective-permute-start(bf16[512,1024]{1,0:T(8,128)(2,1)} %get-tuple-element.14.refs_1_), channel_id=1, source_target_pairs={{0,6},{1,7},{2,0},{3,1},{4,2},{5,3},{6,4},{7,5},{8,14},{9,15},{10,... | collective-permute-start | bytes 3145736 | tf_op jit(solution)/shard_map/ppermute | solution.py:20
  103.9 34.3 %collective-permute-start.20 = (bf16[512,1024]{1,0:T(8,128)(2,1)}, bf16[512,1024]{1,0:T(8,128)(2,1)}, u32[]{:S(2)}, u32[]{:S(2)}) collective-permute-start(bf16[512,1024]{1,0:T(8,128)(2,1)} %get-tuple-element.15.refs_1_), channel_id=1, source_target_pairs={{0,2},{1,3},{2,4},{3,5},{4,6},{5,7},{6,0},{7,1},{8,10},{9,11},{10,... | collective-permute-start | bytes 3145736 | tf_op jit(solution)/shard_map/ppermute | solution.py:20
  105.6 32.6 %collective-permute-start.19 = (bf16[512,1024]{1,0:T(8,128)(2,1)}, bf16[512,1024]{1,0:T(8,128)(2,1)}, u32[]{:S(2)}, u32[]{:S(2)}) collective-permute-start(bf16[512,1024]{1,0:T(8,128)(2,1)} %get-tuple-element.15.refs_1_), channel_id=1, source_target_pairs={{0,6},{1,7},{2,0},{3,1},{4,2},{5,3},{6,4},{7,5},{8,14},{9,15},{10,... | collective-permute-start | bytes 3145736 | tf_op jit(solution)/shard_map/ppermute | solution.py:20
  107.4 27.9 %collective-permute-start.14 = (bf16[4,128,768]{2,1,0:T(8,128)(2,1)}, bf16[4,128,768]{2,1,0:T(8,128)(2,1)S(1)}, u32[]{:S(2)}, u32[]{:S(2)}) collective-permute-start(bf16[4,128,768]{2,1,0:T(8,128)(2,1)} %copy-done.9), channel_id=1, source_target_pairs={{0,8},{8,16},{16,24},{24,32},{32,40},{40,48},{48,56},{56,0},{64,72... | collective-permute-start | bytes 2359304 | tf_op jit(solution)/shard_map/ppermute | solution.py:31
  107.4 28.0 %collective-permute-start.15 = (bf16[4,128,768]{2,1,0:T(8,128)(2,1)}, bf16[4,128,768]{2,1,0:T(8,128)(2,1)S(1)}, u32[]{:S(2)}, u32[]{:S(2)}) collective-permute-start(bf16[4,128,768]{2,1,0:T(8,128)(2,1)} %copy-done.11), channel_id=1, source_target_pairs={{0,56},{8,0},{16,8},{24,16},{32,24},{40,32},{48,40},{56,48},{64,12... | collective-permute-start | bytes 2359304 | tf_op jit(solution)/shard_map/ppermute | solution.py:31
  110.2 1.2 copy-start.2
  111.4 1.2 copy-start.4
  127.5 66.3 %collective-permute-start.29 = (f32[1024,896]{1,0:T(8,128)}, f32[1024,896]{1,0:T(8,128)}, u32[]{:S(2)}, u32[]{:S(2)}) collective-permute-start(f32[1024,896]{1,0:T(8,128)} %get-tuple-element.13), channel_id=1, source_target_pairs={{0,1},{1,0},{2,3},{3,2},{4,5},{5,4},{6,7},{7,6},{8,9},{9,8},{10,11... | collective-permute-start | bytes 11010056 | tf_op jit(solution)/shard_map/ppermute | solution.py:24
  135.3 19.9 %copy-start.6 = (bf16[4,128,768]{2,1,0:T(8,128)(2,1)S(1)}, bf16[4,128,768]{2,1,0:T(8,128)(2,1)}, u32[]{:S(2)}) copy-start(bf16[4,128,768]{2,1,0:T(8,128)(2,1)} %copy-done.5) | copy-start | bytes 2359300
  135.3 19.9 %copy-start.8 = (bf16[4,128,768]{2,1,0:T(8,128)(2,1)S(1)}, bf16[4,128,768]{2,1,0:T(8,128)(2,1)}, u32[]{:S(2)}) copy-start(bf16[4,128,768]{2,1,0:T(8,128)(2,1)} %copy-done.7) | copy-start | bytes 2359300
  135.3 18.4 %copy-start.24 = (bf16[4,128,768]{2,1,0:T(8,128)(2,1)}, bf16[4,128,768]{2,1,0:T(8,128)(2,1)S(1)}, u32[]{:S(2)}) copy-start(bf16[4,128,768]{2,1,0:T(8,128)(2,1)S(1)} %collective-permute-done.14.refs_12_) | copy-start | bytes 2359300
  135.4 14.8 %collective-permute-start.3 = (bf16[256,1024]{1,0:T(8,128)(2,1)S(1)}, bf16[256,1024]{1,0:T(8,128)(2,1)S(1)}, u32[]{:S(2)}, u32[]{:S(2)}) collective-permute-start(bf16[256,1024]{1,0:T(8,128)(2,1)S(1)} %slice.134), channel_id=1, source_target_pairs={{0,2},{1,3},{2,4},{3,5},{4,6},{5,7},{6,0},{7,1},{8,10},{9,11},{10,... | collective-permute-start | bytes 1572872 | tf_op jit(solution)/shard_map/ppermute | solution.py:20
  135.5 18.3 %copy-start.25 = (bf16[4,128,768]{2,1,0:T(8,128)(2,1)}, bf16[4,128,768]{2,1,0:T(8,128)(2,1)S(1)}, u32[]{:S(2)}) copy-start(bf16[4,128,768]{2,1,0:T(8,128)(2,1)S(1)} %collective-permute-done.15.refs_13_) | copy-start | bytes 2359300
  135.5 14.7 %collective-permute-start.4 = (bf16[256,1024]{1,0:T(8,128)(2,1)S(1)}, bf16[256,1024]{1,0:T(8,128)(2,1)S(1)}, u32[]{:S(2)}, u32[]{:S(2)}) collective-permute-start(bf16[256,1024]{1,0:T(8,128)(2,1)S(1)} %slice.135), channel_id=1, source_target_pairs={{0,6},{1,7},{2,0},{3,1},{4,2},{5,3},{6,4},{7,5},{8,14},{9,15},{10,... | collective-permute-start | bytes 1572872 | tf_op jit(solution)/shard_map/ppermute | solution.py:20
  138.2 15.5 %collective-permute-start.16 = (bf16[2,128,768]{2,1,0:T(8,128)(2,1)S(1)}, bf16[2,128,768]{2,1,0:T(8,128)(2,1)S(1)}, u32[]{:S(2)}, u32[]{:S(2)}) collective-permute-start(bf16[2,128,768]{2,1,0:T(8,128)(2,1)S(1)} %slice.140), channel_id=1, source_target_pairs={{0,8},{8,16},{16,24},{24,32},{32,40},{40,48},{48,56},{56,0},{64,72... | collective-permute-start | bytes 1179656 | tf_op jit(solution)/shard_map/ppermute | solution.py:31
  138.3 16.2 %collective-permute-start.17 = (bf16[2,128,768]{2,1,0:T(8,128)(2,1)S(1)}, bf16[2,128,768]{2,1,0:T(8,128)(2,1)S(1)}, u32[]{:S(2)}, u32[]{:S(2)}) collective-permute-start(bf16[2,128,768]{2,1,0:T(8,128)(2,1)S(1)} %slice.141), channel_id=1, source_target_pairs={{0,56},{8,0},{16,8},{24,16},{32,24},{40,32},{48,40},{56,48},{64,12... | collective-permute-start | bytes 1179656 | tf_op jit(solution)/shard_map/ppermute | solution.py:31
  150.2 25.8 %collective-permute-start.21 = (bf16[256,1024]{1,0:T(8,128)(2,1)}, bf16[256,1024]{1,0:T(8,128)(2,1)}, u32[]{:S(2)}, u32[]{:S(2)}) collective-permute-start(bf16[256,1024]{1,0:T(8,128)(2,1)} %slice.144), channel_id=1, source_target_pairs={{0,2},{1,3},{2,4},{3,5},{4,6},{5,7},{6,0},{7,1},{8,10},{9,11},{10,... | collective-permute-start | bytes 1572872 | tf_op jit(solution)/shard_map/ppermute | solution.py:20
  151.0 24.9 %collective-permute-start.22 = (bf16[256,1024]{1,0:T(8,128)(2,1)}, bf16[256,1024]{1,0:T(8,128)(2,1)}, u32[]{:S(2)}, u32[]{:S(2)}) collective-permute-start(bf16[256,1024]{1,0:T(8,128)(2,1)} %slice.145), channel_id=1, source_target_pairs={{0,6},{1,7},{2,0},{3,1},{4,2},{5,3},{6,4},{7,5},{8,14},{9,15},{10,... | collective-permute-start | bytes 1572872 | tf_op jit(solution)/shard_map/ppermute | solution.py:20
  160.6 15.4 %copy-start.19 = (bf16[2,128,768]{2,1,0:T(8,128)(2,1)S(1)}, bf16[2,128,768]{2,1,0:T(8,128)(2,1)}, u32[]{:S(2)}) copy-start(bf16[2,128,768]{2,1,0:T(8,128)(2,1)} %copy-done.17) | copy-start | bytes 1179652
  174.5 15.9 %copy-start.26 = (s32[1024]{0:T(1024)S(1)}, s32[1024]{0:T(1024)}, u32[]{:S(2)}) copy-start(s32[1024]{0:T(1024)} %param.14) | copy-start | bytes 12292
  174.5 19.2 %copy-start.27 = (bf16[512]{0:T(512)(128)(2,1)S(1)}, bf16[512]{0:T(512)(128)(2,1)}, u32[]{:S(2)}) copy-start(bf16[512]{0:T(512)(128)(2,1)} %param.22) | copy-start | bytes 3076
  174.5 29.5 %collective-permute-start.18 = (f32[512,896]{1,0:T(8,128)}, f32[512,896]{1,0:T(8,128)}, u32[]{:S(2)}, u32[]{:S(2)}) collective-permute-start(f32[512,896]{1,0:T(8,128)} %get-tuple-element.9), channel_id=1, source_target_pairs={{0,1},{1,0},{2,3},{3,2},{4,5},{5,4},{6,7},{7,6},{8,9},{9,8},{10,11... | collective-permute-start | bytes 5505032 | tf_op jit(solution)/shard_map/ppermute | solution.py:24
  190.2 20.0 %collective-permute-start.23 = (f32[512,896]{1,0:T(8,128)}, f32[512,896]{1,0:T(8,128)S(1)}, u32[]{:S(2)}, u32[]{:S(2)}) collective-permute-start(f32[512,896]{1,0:T(8,128)} %get-tuple-element.11), channel_id=1, source_target_pairs={{0,1},{1,0},{2,3},{3,2},{4,5},{5,4},{6,7},{7,6},{8,9},{9,8},{10,11... | collective-permute-start | bytes 5505032 | tf_op jit(solution)/shard_map/ppermute | solution.py:24
  194.3 9.7 %copy-start.28 = (bf16[512]{0:T(512)(128)(2,1)S(1)}, bf16[512]{0:T(512)(128)(2,1)}, u32[]{:S(2)}) copy-start(bf16[512]{0:T(512)(128)(2,1)} %param.21) | copy-start | bytes 3076
  210.2 7.6 %slice-start = ((f32[8,1024]{1,0:T(8,128)}), f32[1,1024]{1,0:T(1,128)S(1)}, s32[]{:S(2)}) async-start(f32[8,1024]{1,0:T(8,128)} %shard_map.127), calls=%async_computation.1 | async-start | bytes 8192 | tf_op jit(solution)/shard_map/slice | solution.py:295
  210.2 7.6 %slice-start.1 = ((f32[8,512]{1,0:T(8,128)}), f32[1,512]{1,0:T(1,128)S(1)}, s32[]{:S(2)}) async-start(f32[8,512]{1,0:T(8,128)} %shard_map.123), calls=%async_computation.2 | async-start | bytes 4096 | tf_op jit(solution)/shard_map/slice | solution.py:329
  210.2 1.3 copy-start.23
  (14 other events, 13.1 us)
Sparse Core Ops, SparseCore 0:
  10.9 108.2 all-gather.1

commit v2 on v0

v2 whole, which is shorter than its diff:
```python
import functools

import jax
import jax.numpy as jnp
from jax import lax
from jax.experimental import pallas as pl
from jax.experimental.pallas import tpu as pltpu
from jax.sharding import PartitionSpec as P

HD = 128
NX = 4
WIDE = 768
EPS = 1e-05
BF = jnp.bfloat16
F32 = jnp.float32
EVERY = slice(None)


def shift_x(v, k):
    pairs = [(2 * x + c, 2 * ((x + k) % NX) + c) for x in range(NX) for c in range(2)]
    return lax.ppermute(v, "tp", pairs)


def swap_core(v):
    return lax.ppermute(v, "tp", [(t, t ^ 1) for t in range(2 * NX)])


def over_tp(v):
    v = v + swap_core(v)
    return v + shift_x(v, 1) + (shift_x(v, 2) + shift_x(v, 3))


def step_one(v):
    return shift_x(v, 1), shift_x(v, -1)


def step_two(before, after):
    half = before.shape[0] // 2
    return shift_x(before[:half], 1), shift_x(after[half:], -1)


def aligned(value, step):
    return pl.multiple_of(value, step)


def cheap():
    return pl.CostEstimate(flops=1024, bytes_accessed=1024, transcendentals=0)


def attend_tiles(acc, squares, depth, seg_ref, read_ref, more_ref, out_ref):
    tile = 128
    jds = lax.broadcasted_iota(jnp.int32, (tile, tile), 0)
    ids = lax.broadcasted_iota(jnp.int32, (tile, tile), 1)

    @pl.loop(0, acc.shape[0] // tile // 2)
    def _(pair):
        for u in range(2):
            at = pl.ds(aligned((pair * 2 + u) * tile, tile), tile)
            part = acc[at, :].astype(BF)
            queries = jnp.concatenate([part[:, h * HD : (h + 1) * HD] for h in range(4)], axis=0)
            keys, values = part[:, 4 * HD : 5 * HD], part[:, 5 * HD :]
            segs = jnp.broadcast_to(seg_ref[:, at], (tile, tile))
            allowed = (jds <= ids) & (segs.T == segs)
            mean = jnp.sum(squares[at, :], axis=-1, keepdims=True) * (1.0 / depth)
            key_scale = jnp.broadcast_to(lax.rsqrt(mean + EPS), (tile, tile))
            both = key_scale * key_scale.T * HD ** (-0.5)
            scores = lax.dot_general(
                keys, queries, (((1,), (1,)), ((), ())), preferred_element_type=F32
            )
            hidden = jnp.concatenate([jnp.where(allowed, 0.0, -1e30)] * 4, axis=1) < 0.0
            masked = jnp.where(hidden, -1e30, scores * jnp.concatenate([both] * 4, axis=1))
            powers = jnp.exp(masked - jnp.max(masked, axis=0, keepdims=True))
            inverse = 1.0 / jnp.sum(powers, axis=0, keepdims=True)
            weights = (powers * inverse * jnp.concatenate([key_scale] * 4, axis=1)).astype(BF)
            mixture = lax.dot_general(
                values, weights, (((0,), (0,)), ((), ())), preferred_element_type=F32
            ).astype(BF)
            total = jnp.zeros((8, tile), F32)
            for h in range(4):
                total += jnp.dot(
                    read_ref[h], mixture[:, h * tile : (h + 1) * tile], preferred_element_type=F32
                )
            if more_ref is not None:
                total += more_ref[:, at]
            out_ref[:, at] = total


def start_copies(pos, src, dst, sem, place):
    condition, copies = place(pos)

    def start():
        for from_, to in copies:
            pltpu.make_async_copy(src.at[from_], dst.at[to], sem).start()

    if condition is None:
        start()
    else:
        pl.when(condition)(start)


def project_kernel(plan_x, plan_w, n_x, n_w, prior, finish, *refs):
    pos, refs = refs[0], refs[1:]
    xs, ws, refs = refs[:n_x], refs[n_x : n_x + n_w], refs[n_x + n_w :]
    if prior:
        prior_squares, refs = refs[0], refs[1:]
    if finish:
        seg_ref, read_ref, refs = refs[0], refs[1], refs[2:]
        more_ref, refs = (refs[0], refs[1:]) if finish[1] else (None, refs)
        out_ref, xbuf, wbuf, sems, acc, squares = refs
    else:
        acc, squares, xbuf, wbuf, sems = refs
    slots, rows, width = xbuf.shape
    for slot in range(slots):
        for plan, sources, dst, kind in ((plan_x, xs, xbuf, 0), (plan_w, ws, wbuf, 1)):
            for which, place in plan[slot]:
                start_copies(pos, sources[which], dst.at[slot], sems.at[kind, slot], place)
    acc[...] = jnp.zeros(acc.shape, F32)
    squares[...] = prior_squares[...] if prior else jnp.zeros(squares.shape, F32)

    @pl.loop(0, slots)
    def _(s):
        pltpu.make_async_copy(xbuf.at[s], xbuf.at[s], sems.at[0, s]).wait()

        @pl.when((s == 2) | (not prior))
        def _():
            @pl.loop(0, rows // 64)
            def _(m):
                at = pl.ds(aligned(m * 64, 64), 64)
                total = squares[at, :]
                for k in range(0, width, 128):
                    part = xbuf[s, at, k : k + 128].astype(F32)
                    total += part * part
                squares[at, :] = total

        pltpu.make_async_copy(wbuf.at[s], wbuf.at[s], sems.at[1, s]).wait()

        @pl.loop(0, rows // 512)
        def _(m):
            at = pl.ds(aligned(m * 512, 512), 512)
            for k in range(0, width, 1024):
                acc[at, :] += jnp.dot(
                    xbuf[s, at, k : k + 1024], wbuf[s, k : k + 1024, :], preferred_element_type=F32
                )

    if finish:
        attend_tiles(acc, squares, finish[0], seg_ref, read_ref, more_ref, out_ref)


def project(pos, xs, ws, plan_x, plan_w, width, rows, prior=(), finish=None):
    slots = len(plan_x)
    vmem = pl.BlockSpec(memory_space=pltpu.VMEM)
    operands = [pos] + [
        pltpu.with_memory_space_constraint(v, pltpu.MemorySpace.HBM) for v in (*xs, *ws)
    ]
    specs = [pl.BlockSpec(memory_space=pltpu.SMEM)]
    specs += [pl.BlockSpec(memory_space=pltpu.MemorySpace.HBM)] * (len(xs) + len(ws))
    operands += prior
    specs += [vmem] * len(prior)
    scratch = [
        pltpu.VMEM((slots, rows, width), BF),
        pltpu.VMEM((slots, width, WIDE), BF),
        pltpu.SemaphoreType.DMA((2, slots)),
    ]
    out = (jax.ShapeDtypeStruct((rows, WIDE), F32), jax.ShapeDtypeStruct((rows, 128), F32))
    static = None
    if finish:
        index, depth, segments, readout, more = finish
        at_row = (jnp.arange(8) == index)[None, :, None]
        read = jnp.where(at_row, readout.reshape(4, 1, HD), jnp.zeros((), BF))
        extra = [segments, read] + ([more] if more is not None else [])
        operands += extra
        specs += [vmem] * len(extra)
        scratch += [pltpu.VMEM((rows, WIDE), F32), pltpu.VMEM((rows, 128), F32)]
        out = jax.ShapeDtypeStruct((8, rows), F32)
        static = (depth, more is not None)
    return pl.pallas_call(
        functools.partial(
            project_kernel, plan_x, plan_w, len(xs), len(ws), len(prior) > 0, static
        ),
        out_shape=out,
        in_specs=specs,
        out_specs=vmem if finish else (vmem, vmem),
        scratch_shapes=scratch,
        compiler_params=pltpu.CompilerParams(vmem_limit_bytes=48 * 1024 * 1024),
        cost_estimate=cheap(),
    )(*operands)


def origin(pos, ahead):
    return lax.rem(pos[0] + ahead, NX)


def side(pos, other):
    return 1 - pos[1] if other else pos[1]


def critic_rows_plan(which, other, rows):
    def place(pos):
        to = (pl.ds(*rows), pl.ds(aligned(side(pos, other) * 512, 512), 512))
        return None, [((EVERY, EVERY), to)]

    return [(which, place)]


def critic_weights(ahead):
    plan = []
    for which, (lane, size) in enumerate(((0, 512), (512, 128), (640, 128))):

        def place(pos, lane=lane, size=size):
            rows = pl.ds(aligned(origin(pos, ahead) * 1024, 1024), 1024)
            return None, [((rows, EVERY), (EVERY, pl.ds(lane, size)))]

        plan.append((which, place))
    return plan


def ref_rows_plan(which, other, rows):
    def place(pos):
        to = (pl.ds(*rows), pl.ds(aligned(side(pos, other) * 1024, 1024), 1024))
        return None, [((EVERY, EVERY), to)]

    return [(which, place)]


def gathered_weights(which, ahead):
    def place(pos):
        rows = pl.ds(aligned(origin(pos, ahead) * 2048, 2048), 2048)
        return None, [((rows, EVERY), (EVERY, EVERY))]

    return [(which, place)]


def squares_kernel(*refs):
    xs, out_ref = refs[:-1], refs[-1]

    @pl.loop(0, out_ref.shape[0] // 64)
    def _(m):
        at = pl.ds(aligned(m * 64, 64), 64)
        total = jnp.zeros((64, 128), F32)
        for block in xs:
            for k in range(0, block.shape[1], 128):
                part = block[at, k : k + 128].astype(F32)
                total += part * part
        out_ref[at, :] = total


def squares(xs):
    rows, tile = xs[0].shape[0], 256
    return pl.pallas_call(
        squares_kernel,
        grid=(rows // tile,),
        out_shape=jax.ShapeDtypeStruct((rows, 128), F32),
        in_specs=[pl.BlockSpec((tile, v.shape[1]), lambda i: (i, 0)) for v in xs],
        out_specs=pl.BlockSpec((tile, 128), lambda i: (i, 0)),
        cost_estimate=cheap(),
    )(*[pltpu.with_memory_space_constraint(v, pltpu.MemorySpace.HBM) for v in xs])


def body(
    reference_rows,
    critic_rows,
    segment_ids,
    pack_dest,
    ref_query,
    ref_key,
    ref_value,
    critic_query,
    critic_key,
    critic_value,
    ref_readout,
    critic_readout,
):
    del pack_dest
    tp = lax.axis_index("tp")
    pos = jnp.stack([tp // 2, tp % 2]).astype(jnp.int32)
    seg_row = segment_ids.reshape(1, -1)
    slots = segment_ids.shape[0]
    half = slots // 2

    ref_w = jnp.concatenate([ref_query, ref_key, ref_value], axis=1)
    gathered = lax.all_gather(ref_w, "rep", axis=0, tiled=True)
    critic_before, critic_after = step_one(critic_rows)
    critic_other, ref_other = swap_core(critic_rows), swap_core(reference_rows)

    critic_before, critic_after, critic_other, ref_rows, ref_other = lax.optimization_barrier(
        (critic_before, critic_after, critic_other, reference_rows, ref_other)
    )
    critic_far = step_two(critic_before, critic_after)
    critic_far, ref_rows = lax.optimization_barrier((critic_far, ref_rows))
    ref_before, ref_after = step_one(ref_rows)
    critic_x = [critic_rows, critic_other]
    for v in (critic_after, critic_before, *critic_far):
        critic_x += [v, swap_core(v)]
    plan_x = [[], [], [], []]
    order = ((0, (0, slots)), (1, (0, slots)), (3, (0, slots)), (2, (0, half)), (2, (half, half)))
    for index, (slot, rows) in enumerate(order):
        for other in range(2):
            plan_x[slot] += critic_rows_plan(2 * index + other, other == 1, rows)
    critic_part = project(
        pos,
        critic_x,
        [critic_query, critic_key, critic_value],
        plan_x,
        [critic_weights(k) for k in range(NX)],
        1024,
        slots,
        finish=(1, 4096, seg_row, critic_readout, None),
    )

    ref_before, ref_after, critic_part = lax.optimization_barrier(
        (ref_before, ref_after, critic_part)
    )
    far = step_two(ref_before, ref_after)
    ref_x = [ref_rows, ref_other]
    for v in (ref_after, ref_before):
        ref_x += [v, swap_core(v)]
    total = squares(ref_x)
    far, total = lax.optimization_barrier((far, total))
    for v in far:
        ref_x += [v, swap_core(v)]
    plan_x = [[], [], [], []]
    for index, (slot, rows) in enumerate(order):
        for other in range(2):
            plan_x[slot] += ref_rows_plan(2 * index + other, other == 1, rows)
    partial = project(
        pos,
        ref_x,
        [gathered],
        plan_x,
        [gathered_weights(0, k) for k in range(NX)],
        2048,
        slots,
        prior=(total,),
        finish=(0, 8192, seg_row, ref_readout, critic_part),
    )
    scores = over_tp(partial)
    scores = jnp.where(seg_row >= 0, scores, 0.0)
    return scores[0], scores[1]


def solution(mesh):
    return jax.shard_map(
        body,
        mesh=mesh,
        in_specs=(
            P("rep", "tp"),
            P("rep", "tp"),
            P("rep"),
            P("rep", None),
            P("rep", "tp"),
            P("rep", "tp"),
            P("rep", "tp"),
            P(None, "tp"),
            P(None, "tp"),
            P(None, "tp"),
            P("tp"),
            P("tp"),
        ),
        out_specs=(P("rep"), P("rep")),
        check_vma=False,
    )
```

time: 519 us -> 179 us (0.34)
  waiting for transfers between devices: 287 us -> 85 us
  blocking collectives: 75.1 us -> 0 us
  matrix products: 52.9 us -> 0 us
  Pallas kernels: 0 us -> 46.2 us
  local copies, waits for them, and re-layouts: 31.6 us -> 7.69 us
  other arithmetic: 24.5 us -> 2.06 us
    all_gather x5 -> x1, waiting for transfers between devices: 241 us -> 0.01 us  [body(): gathered = lax.all_gather(ref_w, 'rep', axis=0, tiled=True)]
    ppermute x0 -> x22, waiting for transfers between devices: none -> 85 us  [the longest x11 74.7 us: shift_x(): return lax.ppermute(v, 'tp', pairs)]
    all_to_all x1 -> x0, blocking collectives: 55.1 us -> none  [body(): lax.all_to_all(by_pack(reference_rows), 'rep', split_axis=0, concat_axis=...]
    dot_general x8 -> x0, matrix products: 52.9 us -> none  [the longest x2 19.7 us: attend(): jnp.einsum('pgjd,qgd->gjpq', query_four, key_three, preferred_element_typ...]
    pallas_call x0 -> x3, Pallas kernels: none -> 46.2 us  [the longest x2 39.2 us: project(): pl.pallas_call(functools.partial(project_kernel, plan_x, plan_w, len(xs),...]
    all_to_all x4 -> x0, waiting for transfers between devices: 43.9 us -> none  [the longest x1 19.6 us: body(): lax.all_to_all(ref_spread, 'rep', split_axis=0, concat_axis=0, tiled=True)]
    all_to_all x4 -> x0, starting transfers between devices: 27.9 us -> none  [the longest x1 12 us: body(): lax.all_to_all(by_pack(segment_ids), 'rep', split_axis=0, concat_axis=0,...]
    ppermute x0 -> x22, starting transfers between devices: none -> 23.4 us  [the longest x11 12.2 us: swap_core(): return lax.ppermute(v, 'tp', [(t, t ^ 1) for t in range(2 * NX)])]
  transfers between devices with their start and end apart: 9 -> 23, of which waited for: 7 -> 15; matrix products, arithmetic and copies ran while one was open for 19% -> 2% of each run, Pallas kernels for 0% -> 13%
where the time goes in v2:
time: 179 us
  waiting for transfers between devices  85 us (47%)
  Pallas kernels  46.2 us (26%)
  starting transfers between devices  23.5 us (13%)
  between operations  14.1 us (8%)
  local copies, waits for them, and re-layouts  7.69 us (4%)
  other arithmetic  2.06 us (1%)
    ppermute x11, waiting for transfers between devices, shift_x(): return lax.ppermute(v, 'tp', pairs)  74.7 us
    pallas_call x2, Pallas kernels, project(): pl.pallas_call(functools.partial(project_kernel, plan_x, plan_w, len(xs),...  39.2 us
    ppermute x11, starting transfers between devices, swap_core(): return lax.ppermute(v, 'tp', [(t, t ^ 1) for t in range(2 * NX)])  12.2 us
    ppermute x11, starting transfers between devices, shift_x(): return lax.ppermute(v, 'tp', pairs)  11.2 us
    ppermute x11, waiting for transfers between devices, swap_core(): return lax.ppermute(v, 'tp', [(t, t ^ 1) for t in range(2 * NX)])  10.3 us
    pallas_call x1, Pallas kernels, squares(): pl.pallas_call(squares_kernel, grid=(rows // tile,), out_shape=jax.ShapeD...  7.03 us
    slice x4, local copies, waits for them, and re-layouts, step_two(): return (shift_x(before[:half], 1), shift_x(after[half:], -1))  3.6 us
  transfers between devices with their start and end apart: 23, of which 15 were waited for; matrix products, arithmetic and copies ran while one was open for 2% of the time, Pallas kernels for 13%

profile of v2, /device:TPU:1, one launch (start us, length us, event | category | flops | bytes accessed | tf_op | source)
XLA Modules:
  0.0 178.6 jit_solution(821307239687692615)
XLA Ops:
  7.2 0.0 all-gather.2.cloned.1.call-start
  7.2 1.8 %pad_maximum_fusion = bf16[256,768]{1,0:T(8,128)(2,1)} fusion(bf16[256,128]{1,0:T(8,128)(2,1)} %param.17, bf16[256,128]{1,0:T(8,128)(2,1)} %param.16, bf16[256,512]{1,0:T(8,128)(2,1)} %param.15), kind=kLoop, calls=%fused_computation | loop fusion | flops 1179648 | bytes 786432 | tf_op jit(solution)/shard_map/concatenate | solution.py:280
  9.0 0.0 all-gather.2.cloned.1.call-update
  9.1 3.3 %collective-permute-start.3 = (bf16[1024,1024]{1,0:T(8,128)(2,1)}, bf16[1024,1024]{1,0:T(8,128)(2,1)}, u32[]{:S(2)}, u32[]{:S(2)}) collective-permute-start(bf16[1024,1024]{1,0:T(8,128)(2,1)} %refs_1_.2), channel_id=1, source_target_pairs={{0,1},{1,0},{2,3},{3,2},{4,5},{5,4},{6,7},{7,6},{8,9},{9,8},{10,11... | collective-permute-start | bytes 6291464 | tf_op jit(solution)/shard_map/ppermute | solution.py:25
  12.4 0.8 collective-permute-start.1
  13.1 0.7 collective-permute-start
  13.9 0.6 collective-permute-start.2
  14.5 22.9 %collective-permute-done.1.refs_3_ = bf16[1024,512]{1,0:T(8,128)(2,1)S(1)} collective-permute-done((bf16[1024,512]{1,0:T(8,128)(2,1)}, bf16[1024,512]{1,0:T(8,128)(2,1)S(1)}, u32[]{:S(2)}, u32[]{:S(2)}) %collective-permute-start.1) | collective-permute-done | bytes 1048608 | tf_op jit(solution)/shard_map/ppermute | solution.py:21
  37.4 1.6 collective-permute-done.refs_5_
  39.2 0.3 collective-permute-start.5
  39.5 1.2 collective-permute-start.4
  40.7 11.0 %collective-permute-done.5.refs_9_ = bf16[512,512]{1,0:T(8,128)(2,1)} collective-permute-done((bf16[512,512]{1,0:T(8,128)(2,1)S(1)}, bf16[512,512]{1,0:T(8,128)(2,1)}, u32[]{:S(2)}, u32[]{:S(2)}) %collective-permute-start.5) | collective-permute-done | bytes 524320 | tf_op jit(solution)/shard_map/ppermute | solution.py:21
  51.7 1.4 collective-permute-done.4.refs_7_
  53.0 0.3 collective-permute-start.7
  53.3 1.2 collective-permute-start.6
  54.5 2.6 %collective-permute-start.9 = (bf16[1024,512]{1,0:T(8,128)(2,1)S(1)}, bf16[1024,512]{1,0:T(8,128)(2,1)S(1)}, u32[]{:S(2)}, u32[]{:S(2)}) collective-permute-start(bf16[1024,512]{1,0:T(8,128)(2,1)S(1)} %collective-permute-done.refs_5_), channel_id=1, source_target_pairs={{0,1},{1,0},{2,3},{3,2},{4,5},{5,4},{6,7},{7,6},{8,9},{9,8},{10,11... | collective-permute-start | bytes 3145736 | tf_op jit(solution)/shard_map/ppermute | solution.py:25
  57.1 0.5 collective-permute-start.10
  57.7 3.2 %collective-permute-done.9.refs_6_ = bf16[1024,512]{1,0:T(8,128)(2,1)S(1)} collective-permute-done((bf16[1024,512]{1,0:T(8,128)(2,1)S(1)}, bf16[1024,512]{1,0:T(8,128)(2,1)S(1)}, u32[]{:S(2)}, u32[]{:S(2)}) %collective-permute-start.9) | collective-permute-done | bytes 1048608 | tf_op jit(solution)/shard_map/ppermute | solution.py:25
  60.9 1.0 copy-done.6
  61.9 0.4 collective-permute-start.11
  62.3 0.1 pad_add_fusion.refs_0_
  62.4 0.1 broadcast_select_fusion.1.refs_15_
  62.5 1.7 collective-permute-done.11.refs_10_
  64.2 15.8 %shard_map.122.refs_15_ = f32[8,1024]{1,0:T(8,128)S(1)} custom-call(s32[2]{0:T(128)S(1)} %pad_add_fusion.refs_0_, bf16[1024,512]{1,0:T(8,128)(2,1)} %refs_1_.1, bf16[1024,512]{1,0:T(8,128)(2,1)} %collective-permute-done.2.refs_2_, bf16[1024,512]{1,0:T(8,128)(2,1)} %copy-done.4, bf16[1024,512]{1,0:T(8,128)(2,1)} %collective-permute-done.8.refs_4_, ...), custom_call_target="tpu_custom_call" | custom-call | flops 1024 | bytes 1024 | tf_op jit(solution)/shard_map/pallas_call | solution.py:176
  79.9 18.5 %collective-permute-done.7.refs_2_.refs_3_ = bf16[1024,1024]{1,0:T(8,128)(2,1)S(1)} collective-permute-done((bf16[1024,1024]{1,0:T(8,128)(2,1)}, bf16[1024,1024]{1,0:T(8,128)(2,1)S(1)}, u32[]{:S(2)}, u32[]{:S(2)}) %collective-permute-start.7) | collective-permute-done | bytes 2097184 | tf_op jit(solution)/shard_map/ppermute | solution.py:21
  98.4 1.5 collective-permute-done.6.refs_4_.refs_5_
  99.9 3.0 %collective-permute-start.12 = (bf16[1024,1024]{1,0:T(8,128)(2,1)S(1)}, bf16[1024,1024]{1,0:T(8,128)(2,1)S(1)}, u32[]{:S(2)}, u32[]{:S(2)}) collective-permute-start(bf16[1024,1024]{1,0:T(8,128)(2,1)S(1)} %collective-permute-done.7.refs_2_.refs_3_), channel_id=1, source_target_pairs={{0,1},{1,0},{2,3},{3,2},{4,5},{5,4},{6,7},{7,6},{8,9},{9,8},{10,11... | collective-permute-start | bytes 6291464 | tf_op jit(solution)/shard_map/ppermute | solution.py:25
  102.9 1.1 slice.21
  104.0 2.4 %slice.20 = bf16[512,1024]{1,0:T(8,128)(2,1)} slice(bf16[1024,1024]{1,0:T(8,128)(2,1)} %collective-permute-done.6.refs_4_.refs_5_), slice={[0:512], [0:1024]} | slice | bytes 2097152 | tf_op jit(solution)/shard_map/slice | solution.py:39
  106.5 2.7 %collective-permute-start.15 = (bf16[512,1024]{1,0:T(8,128)(2,1)}, bf16[512,1024]{1,0:T(8,128)(2,1)}, u32[]{:S(2)}, u32[]{:S(2)}) collective-permute-start(bf16[512,1024]{1,0:T(8,128)(2,1)} %slice.21), channel_id=1, source_target_pairs={{0,6},{1,7},{2,0},{3,1},{4,2},{5,3},{6,4},{7,5},{8,14},{9,15},{10,... | collective-permute-start | bytes 3145736 | tf_op jit(solution)/shard_map/ppermute | solution.py:21
  109.1 0.5 collective-permute-done.12.refs_3_.refs_4_
  109.7 1.4 copy-done.3
  111.1 7.0 %shard_map.123.refs_12_ = f32[1024,128]{1,0:T(8,128)} custom-call(bf16[1024,1024]{1,0:T(8,128)(2,1)} %refs_1_.2, bf16[1024,1024]{1,0:T(8,128)(2,1)} %collective-permute-done.3.refs_1_.refs_2_, bf16[1024,1024]{1,0:T(8,128)(2,1)} %copy-done.2, bf16[1024,1024]{1,0:T(8,128)(2,1)} %copy-done.3, bf16[1024,1024]{1,0:T(8,128)(2,1)} %collective-permute-done.6.refs_4_.refs_5_, ...), custom_call_target="tpu_custom_call" | custom-call | flops 1024 | bytes 1024 | tf_op jit(solution)/shard_map/pallas_call | solution.py:249
  118.1 14.2 %collective-permute-done.14.refs_7_ = bf16[512,1024]{1,0:T(8,128)(2,1)S(1)} collective-permute-done((bf16[512,1024]{1,0:T(8,128)(2,1)}, bf16[512,1024]{1,0:T(8,128)(2,1)S(1)}, u32[]{:S(2)}, u32[]{:S(2)}) %collective-permute-start.14) | collective-permute-done | bytes 1048608 | tf_op jit(solution)/shard_map/ppermute | solution.py:21
  132.3 1.2 collective-permute-start.16
  133.5 0.1 collective-permute-start.17
  133.6 0.1 broadcast_select_fusion.refs_14_
  133.6 2.7 %collective-permute-done.16.refs_8_ = bf16[512,1024]{1,0:T(8,128)(2,1)S(1)} collective-permute-done((bf16[512,1024]{1,0:T(8,128)(2,1)S(1)}, bf16[512,1024]{1,0:T(8,128)(2,1)S(1)}, u32[]{:S(2)}, u32[]{:S(2)}) %collective-permute-start.16) | collective-permute-done | bytes 1048608 | tf_op jit(solution)/shard_map/ppermute | solution.py:25
  136.3 1.3 collective-permute-done.17.refs_10_
  137.6 1.0 copy-done
  138.6 23.4 %shard_map.124 = f32[8,1024]{1,0:T(8,128)S(1)} custom-call(s32[2]{0:T(128)S(1)} %pad_add_fusion.refs_0_, bf16[1024,1024]{1,0:T(8,128)(2,1)} %refs_1_.2, bf16[1024,1024]{1,0:T(8,128)(2,1)} %collective-permute-done.3.refs_1_.refs_2_, bf16[1024,1024]{1,0:T(8,128)(2,1)} %copy-done.2, bf16[1024,1024]{1,0:T(8,128)(2,1)} %copy-done.3, ...), custom_call_target="tpu_custom_call" | custom-call | flops 1024 | bytes 1024 | tf_op jit(solution)/shard_map/pallas_call | solution.py:176
  162.1 0.5 collective-permute-start.18
  162.5 0.9 collective-permute-done.18
  163.4 3.4 %collective-permute-start.21 = (f32[8,1024]{1,0:T(8,128)S(1)}, f32[8,1024]{1,0:T(8,128)S(1)}, u32[]{:S(2)}, u32[]{:S(2)}) collective-permute-start(f32[8,1024]{1,0:T(8,128)S(1)} %add.18), channel_id=1, source_target_pairs={{0,6},{1,7},{2,0},{3,1},{4,2},{5,3},{6,4},{7,5},{8,14},{9,15},{10,... | collective-permute-start | bytes 98312 | tf_op jit(solution)/shard_map/ppermute | solution.py:21
  166.8 0.7 collective-permute-start.19
  167.5 0.3 collective-permute-done.21
  167.8 3.3 %collective-permute-done.20 = f32[8,1024]{1,0:T(8,128)S(1)} collective-permute-done((f32[8,1024]{1,0:T(8,128)S(1)}, f32[8,1024]{1,0:T(8,128)S(1)}, u32[]{:S(2)}, u32[]{:S(2)}) %collective-permute-start.20) | collective-permute-done | bytes 32800 | tf_op jit(solution)/shard_map/ppermute | solution.py:21
  171.1 0.6 fusion
  (38 shorter events, 0.2 us)
Async XLA Ops:
  7.2 55.2 %copy-start.9 = (bf16[512]{0:T(512)(128)(2,1)S(1)}, bf16[512]{0:T(512)(128)(2,1)}, u32[]{:S(2)}) copy-start(bf16[512]{0:T(512)(128)(2,1)} %param.22) | copy-start | bytes 3076
  7.2 57.0 %copy-start.1 = (s32[1024]{0:T(1024)S(1)}, s32[1024]{0:T(1024)}, u32[]{:S(2)}) copy-start(s32[1024]{0:T(1024)} %param.14) | copy-start | bytes 12292
  7.2 130.4 %all-gather.2.cloned.1.call-start = ((), (), s32[]{:S(2)}) async-start(), calls=%async_computation | async-start | bytes 12976128 | tf_op jit(solution)/shard_map/all_gather | solution.py:281
  9.1 30.0 %collective-permute-start.3 = (bf16[1024,1024]{1,0:T(8,128)(2,1)}, bf16[1024,1024]{1,0:T(8,128)(2,1)}, u32[]{:S(2)}, u32[]{:S(2)}) collective-permute-start(bf16[1024,1024]{1,0:T(8,128)(2,1)} %refs_1_.2), channel_id=1, source_target_pairs={{0,1},{1,0},{2,3},{3,2},{4,5},{5,4},{6,7},{7,6},{8,9},{9,8},{10,11... | collective-permute-start | bytes 6291464 | tf_op jit(solution)/shard_map/ppermute | solution.py:25
  12.4 25.0 %collective-permute-start.1 = (bf16[1024,512]{1,0:T(8,128)(2,1)}, bf16[1024,512]{1,0:T(8,128)(2,1)S(1)}, u32[]{:S(2)}, u32[]{:S(2)}) collective-permute-start(bf16[1024,512]{1,0:T(8,128)(2,1)} %refs_1_.1), channel_id=1, source_target_pairs={{0,6},{1,7},{2,0},{3,1},{4,2},{5,3},{6,4},{7,5},{8,14},{9,15},{10,... | collective-permute-start | bytes 3145736 | tf_op jit(solution)/shard_map/ppermute | solution.py:21
  13.1 25.9 %collective-permute-start = (bf16[1024,512]{1,0:T(8,128)(2,1)}, bf16[1024,512]{1,0:T(8,128)(2,1)S(1)}, u32[]{:S(2)}, u32[]{:S(2)}) collective-permute-start(bf16[1024,512]{1,0:T(8,128)(2,1)} %refs_1_.1), channel_id=1, source_target_pairs={{0,2},{1,3},{2,4},{3,5},{4,6},{5,7},{6,0},{7,1},{8,10},{9,11},{10,... | collective-permute-start | bytes 3145736 | tf_op jit(solution)/shard_map/ppermute | solution.py:21
  13.9 25.2 %collective-permute-start.2 = (bf16[1024,512]{1,0:T(8,128)(2,1)}, bf16[1024,512]{1,0:T(8,128)(2,1)}, u32[]{:S(2)}, u32[]{:S(2)}) collective-permute-start(bf16[1024,512]{1,0:T(8,128)(2,1)} %refs_1_.1), channel_id=1, source_target_pairs={{0,1},{1,0},{2,3},{3,2},{4,5},{5,4},{6,7},{7,6},{8,9},{9,8},{10,11... | collective-permute-start | bytes 3145736 | tf_op jit(solution)/shard_map/ppermute | solution.py:25
  37.4 26.8 %copy-start.4 = (bf16[1024,512]{1,0:T(8,128)(2,1)}, bf16[1024,512]{1,0:T(8,128)(2,1)S(1)}, u32[]{:S(2)}) copy-start(bf16[1024,512]{1,0:T(8,128)(2,1)S(1)} %collective-permute-done.1.refs_3_) | copy-start | bytes 3145732
  39.1 15.5 %copy-start.5 = (bf16[1024,512]{1,0:T(8,128)(2,1)}, bf16[1024,512]{1,0:T(8,128)(2,1)S(1)}, u32[]{:S(2)}) copy-start(bf16[1024,512]{1,0:T(8,128)(2,1)S(1)} %collective-permute-done.refs_5_) | copy-start | bytes 3145732
  39.2 12.5 %collective-permute-start.5 = (bf16[512,512]{1,0:T(8,128)(2,1)S(1)}, bf16[512,512]{1,0:T(8,128)(2,1)}, u32[]{:S(2)}, u32[]{:S(2)}) collective-permute-start(bf16[512,512]{1,0:T(8,128)(2,1)S(1)} %slice.19), channel_id=1, source_target_pairs={{0,6},{1,7},{2,0},{3,1},{4,2},{5,3},{6,4},{7,5},{8,14},{9,15},{10,... | collective-permute-start | bytes 1572872 | tf_op jit(solution)/shard_map/ppermute | solution.py:21
  39.5 13.6 %collective-permute-start.4 = (bf16[512,512]{1,0:T(8,128)(2,1)S(1)}, bf16[512,512]{1,0:T(8,128)(2,1)}, u32[]{:S(2)}, u32[]{:S(2)}) collective-permute-start(bf16[512,512]{1,0:T(8,128)(2,1)S(1)} %slice.18), channel_id=1, source_target_pairs={{0,2},{1,3},{2,4},{3,5},{4,6},{5,7},{6,0},{7,1},{8,10},{9,11},{10,... | collective-permute-start | bytes 1572872 | tf_op jit(solution)/shard_map/ppermute | solution.py:21
  53.0 45.4 %collective-permute-start.7 = (bf16[1024,1024]{1,0:T(8,128)(2,1)}, bf16[1024,1024]{1,0:T(8,128)(2,1)S(1)}, u32[]{:S(2)}, u32[]{:S(2)}) collective-permute-start(bf16[1024,1024]{1,0:T(8,128)(2,1)} %refs_1_.2), channel_id=1, source_target_pairs={{0,6},{1,7},{2,0},{3,1},{4,2},{5,3},{6,4},{7,5},{8,14},{9,15},{10,... | collective-permute-start | bytes 6291464 | tf_op jit(solution)/shard_map/ppermute | solution.py:21
  53.3 46.6 %collective-permute-start.6 = (bf16[1024,1024]{1,0:T(8,128)(2,1)}, bf16[1024,1024]{1,0:T(8,128)(2,1)}, u32[]{:S(2)}, u32[]{:S(2)}) collective-permute-start(bf16[1024,1024]{1,0:T(8,128)(2,1)} %refs_1_.2), channel_id=1, source_target_pairs={{0,2},{1,3},{2,4},{3,5},{4,6},{5,7},{6,0},{7,1},{8,10},{9,11},{10,... | collective-permute-start | bytes 6291464 | tf_op jit(solution)/shard_map/ppermute | solution.py:21
  54.5 6.4 %collective-permute-start.9 = (bf16[1024,512]{1,0:T(8,128)(2,1)S(1)}, bf16[1024,512]{1,0:T(8,128)(2,1)S(1)}, u32[]{:S(2)}, u32[]{:S(2)}) collective-permute-start(bf16[1024,512]{1,0:T(8,128)(2,1)S(1)} %collective-permute-done.refs_5_), channel_id=1, source_target_pairs={{0,1},{1,0},{2,3},{3,2},{4,5},{5,4},{6,7},{7,6},{8,9},{9,8},{10,11... | collective-permute-start | bytes 3145736 | tf_op jit(solution)/shard_map/ppermute | solution.py:25
  57.1 5.3 %collective-permute-start.8 = (bf16[1024,512]{1,0:T(8,128)(2,1)S(1)}, bf16[1024,512]{1,0:T(8,128)(2,1)}, u32[]{:S(2)}, u32[]{:S(2)}) collective-permute-start(bf16[1024,512]{1,0:T(8,128)(2,1)S(1)} %collective-permute-done.1.refs_3_), channel_id=1, source_target_pairs={{0,1},{1,0},{2,3},{3,2},{4,5},{5,4},{6,7},{7,6},{8,9},{9,8},{10,11... | collective-permute-start | bytes 3145736 | tf_op jit(solution)/shard_map/ppermute | solution.py:25
  57.1 5.3 %collective-permute-start.10 = (bf16[512,512]{1,0:T(8,128)(2,1)}, bf16[512,512]{1,0:T(8,128)(2,1)}, u32[]{:S(2)}, u32[]{:S(2)}) collective-permute-start(bf16[512,512]{1,0:T(8,128)(2,1)} %collective-permute-done.4.refs_7_), channel_id=1, source_target_pairs={{0,1},{1,0},{2,3},{3,2},{4,5},{5,4},{6,7},{7,6},{8,9},{9,8},{10,11... | collective-permute-start | bytes 1572872 | tf_op jit(solution)/shard_map/ppermute | solution.py:25
  60.9 1.0 copy-start.6
  61.9 2.3 %collective-permute-start.11 = (bf16[512,512]{1,0:T(8,128)(2,1)}, bf16[512,512]{1,0:T(8,128)(2,1)}, u32[]{:S(2)}, u32[]{:S(2)}) collective-permute-start(bf16[512,512]{1,0:T(8,128)(2,1)} %collective-permute-done.5.refs_9_), channel_id=1, source_target_pairs={{0,1},{1,0},{2,3},{3,2},{4,5},{5,4},{6,7},{7,6},{8,9},{9,8},{10,11... | collective-permute-start | bytes 1572872 | tf_op jit(solution)/shard_map/ppermute | solution.py:25
  98.4 8.0 %copy-start.2 = (bf16[1024,1024]{1,0:T(8,128)(2,1)}, bf16[1024,1024]{1,0:T(8,128)(2,1)S(1)}, u32[]{:S(2)}) copy-start(bf16[1024,1024]{1,0:T(8,128)(2,1)S(1)} %collective-permute-done.7.refs_2_.refs_3_) | copy-start | bytes 6291460
  99.9 9.7 %collective-permute-start.12 = (bf16[1024,1024]{1,0:T(8,128)(2,1)S(1)}, bf16[1024,1024]{1,0:T(8,128)(2,1)S(1)}, u32[]{:S(2)}, u32[]{:S(2)}) collective-permute-start(bf16[1024,1024]{1,0:T(8,128)(2,1)S(1)} %collective-permute-done.7.refs_2_.refs_3_), channel_id=1, source_target_pairs={{0,1},{1,0},{2,3},{3,2},{4,5},{5,4},{6,7},{7,6},{8,9},{9,8},{10,11... | collective-permute-start | bytes 6291464 | tf_op jit(solution)/shard_map/ppermute | solution.py:25
  102.9 8.1 %collective-permute-start.13 = (bf16[1024,1024]{1,0:T(8,128)(2,1)}, bf16[1024,1024]{1,0:T(8,128)(2,1)}, u32[]{:S(2)}, u32[]{:S(2)}) collective-permute-start(bf16[1024,1024]{1,0:T(8,128)(2,1)} %collective-permute-done.6.refs_4_.refs_5_), channel_id=1, source_target_pairs={{0,1},{1,0},{2,3},{3,2},{4,5},{5,4},{6,7},{7,6},{8,9},{9,8},{10,11... | collective-permute-start | bytes 6291464 | tf_op jit(solution)/shard_map/ppermute | solution.py:25
  106.4 27.1 %copy-start.10 = (bf16[512]{0:T(512)(128)(2,1)S(1)}, bf16[512]{0:T(512)(128)(2,1)}, u32[]{:S(2)}) copy-start(bf16[512]{0:T(512)(128)(2,1)} %param.21) | copy-start | bytes 3076
  106.4 25.8 %collective-permute-start.14 = (bf16[512,1024]{1,0:T(8,128)(2,1)}, bf16[512,1024]{1,0:T(8,128)(2,1)S(1)}, u32[]{:S(2)}, u32[]{:S(2)}) collective-permute-start(bf16[512,1024]{1,0:T(8,128)(2,1)} %slice.20), channel_id=1, source_target_pairs={{0,2},{1,3},{2,4},{3,5},{4,6},{5,7},{6,0},{7,1},{8,10},{9,11},{10,... | collective-permute-start | bytes 3145736 | tf_op jit(solution)/shard_map/ppermute | solution.py:21
  106.5 25.8 %collective-permute-start.15 = (bf16[512,1024]{1,0:T(8,128)(2,1)}, bf16[512,1024]{1,0:T(8,128)(2,1)}, u32[]{:S(2)}, u32[]{:S(2)}) collective-permute-start(bf16[512,1024]{1,0:T(8,128)(2,1)} %slice.21), channel_id=1, source_target_pairs={{0,6},{1,7},{2,0},{3,1},{4,2},{5,3},{6,4},{7,5},{8,14},{9,15},{10,... | collective-permute-start | bytes 3145736 | tf_op jit(solution)/shard_map/ppermute | solution.py:21
  109.7 1.4 copy-start.3
  132.3 5.3 %copy-start.7 = (bf16[512,1024]{1,0:T(8,128)(2,1)}, bf16[512,1024]{1,0:T(8,128)(2,1)S(1)}, u32[]{:S(2)}) copy-start(bf16[512,1024]{1,0:T(8,128)(2,1)S(1)} %collective-permute-done.14.refs_7_) | copy-start | bytes 3145732
  132.3 4.0 %collective-permute-start.16 = (bf16[512,1024]{1,0:T(8,128)(2,1)S(1)}, bf16[512,1024]{1,0:T(8,128)(2,1)S(1)}, u32[]{:S(2)}, u32[]{:S(2)}) collective-permute-start(bf16[512,1024]{1,0:T(8,128)(2,1)S(1)} %collective-permute-done.14.refs_7_), channel_id=1, source_target_pairs={{0,1},{1,0},{2,3},{3,2},{4,5},{5,4},{6,7},{7,6},{8,9},{9,8},{10,11... | collective-permute-start | bytes 3145736 | tf_op jit(solution)/shard_map/ppermute | solution.py:25
  133.5 4.1 %collective-permute-start.17 = (bf16[512,1024]{1,0:T(8,128)(2,1)}, bf16[512,1024]{1,0:T(8,128)(2,1)}, u32[]{:S(2)}, u32[]{:S(2)}) collective-permute-start(bf16[512,1024]{1,0:T(8,128)(2,1)} %collective-permute-done.15.refs_9_), channel_id=1, source_target_pairs={{0,1},{1,0},{2,3},{3,2},{4,5},{5,4},{6,7},{7,6},{8,9},{9,8},{10,11... | collective-permute-start | bytes 3145736 | tf_op jit(solution)/shard_map/ppermute | solution.py:25
  136.3 1.3 copy-start.8
  137.6 1.0 copy-start
  162.1 1.3 collective-permute-start.18
  163.4 4.4 %collective-permute-start.21 = (f32[8,1024]{1,0:T(8,128)S(1)}, f32[8,1024]{1,0:T(8,128)S(1)}, u32[]{:S(2)}, u32[]{:S(2)}) collective-permute-start(f32[8,1024]{1,0:T(8,128)S(1)} %add.18), channel_id=1, source_target_pairs={{0,6},{1,7},{2,0},{3,1},{4,2},{5,3},{6,4},{7,5},{8,14},{9,15},{10,... | collective-permute-start | bytes 98312 | tf_op jit(solution)/shard_map/ppermute | solution.py:21
  166.8 4.3 %collective-permute-start.20 = (f32[8,1024]{1,0:T(8,128)S(1)}, f32[8,1024]{1,0:T(8,128)S(1)}, u32[]{:S(2)}, u32[]{:S(2)}) collective-permute-start(f32[8,1024]{1,0:T(8,128)S(1)} %add.18), channel_id=1, source_target_pairs={{0,4},{1,5},{2,6},{3,7},{4,0},{5,1},{6,2},{7,3},{8,12},{9,13},{10,... | collective-permute-start | bytes 98312 | tf_op jit(solution)/shard_map/ppermute | solution.py:21
  166.8 4.3 %collective-permute-start.19 = (f32[8,1024]{1,0:T(8,128)S(1)}, f32[8,1024]{1,0:T(8,128)S(1)}, u32[]{:S(2)}, u32[]{:S(2)}) collective-permute-start(f32[8,1024]{1,0:T(8,128)S(1)} %add.18), channel_id=1, source_target_pairs={{0,2},{1,3},{2,4},{3,5},{4,6},{5,7},{6,0},{7,1},{8,10},{9,11},{10,... | collective-permute-start | bytes 98312 | tf_op jit(solution)/shard_map/ppermute | solution.py:21
Sparse Core Ops, SparseCore 0:
  10.6 123.1 all-gather.1

commit v3 on v2

--- a/solution.py
+++ b/solution.py
@@ -103,26 +103,29 @@
     xs, ws, refs = refs[:n_x], refs[n_x : n_x + n_w], refs[n_x + n_w :]
     if prior:
         prior_squares, refs = refs[0], refs[1:]
+    prior_ref, refs = (refs[0], refs[1:]) if prior > 1 else (None, refs)
     if finish:
         seg_ref, read_ref, refs = refs[0], refs[1], refs[2:]
         more_ref, refs = (refs[0], refs[1:]) if finish[1] else (None, refs)
         out_ref, xbuf, wbuf, sems, acc, squares = refs
     else:
-        acc, squares, xbuf, wbuf, sems = refs
+        acc, xbuf, wbuf, sems = refs
+        squares = None
     slots, rows, width = xbuf.shape
     for slot in range(slots):
         for plan, sources, dst, kind in ((plan_x, xs, xbuf, 0), (plan_w, ws, wbuf, 1)):
             for which, place in plan[slot]:
                 start_copies(pos, sources[which], dst.at[slot], sems.at[kind, slot], place)
-    acc[...] = jnp.zeros(acc.shape, F32)
-    squares[...] = prior_squares[...] if prior else jnp.zeros(squares.shape, F32)
+    acc[...] = prior_ref[...] if prior > 1 else jnp.zeros(acc.shape, F32)
+    if finish:
+        squares[...] = prior_squares[...] if prior else jnp.zeros(squares.shape, F32)
 
     @pl.loop(0, slots)
     def _(s):
         pltpu.make_async_copy(xbuf.at[s], xbuf.at[s], sems.at[0, s]).wait()
 
-        @pl.when((s == 2) | (not prior))
-        def _():
+        if finish:
+
             @pl.loop(0, rows // 64)
             def _(m):
                 at = pl.ds(aligned(m * 64, 64), 64)
@@ -161,7 +164,7 @@
         pltpu.VMEM((slots, width, WIDE), BF),
         pltpu.SemaphoreType.DMA((2, slots)),
     ]
-    out = (jax.ShapeDtypeStruct((rows, WIDE), F32), jax.ShapeDtypeStruct((rows, 128), F32))
+    out = jax.ShapeDtypeStruct((rows, WIDE), F32)
     static = None
     if finish:
         index, depth, segments, readout, more = finish
@@ -175,11 +178,11 @@
         static = (depth, more is not None)
     return pl.pallas_call(
         functools.partial(
-            project_kernel, plan_x, plan_w, len(xs), len(ws), len(prior) > 0, static
+            project_kernel, plan_x, plan_w, len(xs), len(ws), len(prior), static
         ),
         out_shape=out,
         in_specs=specs,
-        out_specs=vmem if finish else (vmem, vmem),
+        out_specs=vmem,
         scratch_shapes=scratch,
         compiler_params=pltpu.CompilerParams(vmem_limit_bytes=48 * 1024 * 1024),
         cost_estimate=cheap(),
@@ -315,22 +318,34 @@
     for v in (ref_after, ref_before):
         ref_x += [v, swap_core(v)]
     total = squares(ref_x)
-    far, total = lax.optimization_barrier((far, total))
-    for v in far:
-        ref_x += [v, swap_core(v)]
-    plan_x = [[], [], [], []]
-    for index, (slot, rows) in enumerate(order):
+    plan_x = [[], [], []]
+    for index, slot in enumerate(range(3)):
         for other in range(2):
-            plan_x[slot] += ref_rows_plan(2 * index + other, other == 1, rows)
-    partial = project(
+            plan_x[slot] += ref_rows_plan(2 * index + other, other == 1, (0, slots))
+    near = project(
         pos,
         ref_x,
         [gathered],
         plan_x,
-        [gathered_weights(0, k) for k in range(NX)],
+        [gathered_weights(0, k) for k in (0, 1, 3)],
         2048,
         slots,
-        prior=(total,),
+    )
+    far, total = lax.optimization_barrier((far, total))
+    far_x, plan_x = [], [[]]
+    for index, v in enumerate(far):
+        far_x += [v, swap_core(v)]
+        for other in range(2):
+            plan_x[0] += ref_rows_plan(2 * index + other, other == 1, (index * half, half))
+    partial = project(
+        pos,
+        far_x,
+        [gathered],
+        plan_x,
+        [gathered_weights(0, 2)],
+        2048,
+        slots,
+        prior=(total, near),
         finish=(0, 8192, seg_row, ref_readout, critic_part),
     )
     scores = over_tp(partial)

time: 179 us -> 178 us (level)
  waiting for transfers between devices: 85 us -> 77.8 us
  starting transfers between devices: 23.5 us -> 28 us
  Pallas kernels: 46.2 us -> 49.1 us
    ppermute x11, starting transfers between devices: 11.2 us -> 15.9 us  [shift_x(): return lax.ppermute(v, 'tp', pairs)]
    ppermute x11, waiting for transfers between devices: 10.3 us -> 6.22 us  [swap_core(): return lax.ppermute(v, 'tp', [(t, t ^ 1) for t in range(2 * NX)])]
    ppermute x11, waiting for transfers between devices: 74.7 us -> 70.8 us  [shift_x(): return lax.ppermute(v, 'tp', pairs)]
    pallas_call x2 -> x3, Pallas kernels: 39.2 us -> 42.1 us  [project(): pl.pallas_call(functools.partial(project_kernel, plan_x, plan_w, len(xs),...]
  transfers between devices with their start and end apart: 23 -> 23, of which waited for: 15 -> 11; matrix products, arithmetic and copies ran while one was open for 2% -> 2% of each run, Pallas kernels for 13% -> 21%
where the time goes in v3:
time: 178 us; the launch traced here: 177 us
  waiting for transfers between devices  77.8 us (44%)
  Pallas kernels  49.1 us (28%)
  starting transfers between devices  28 us (16%)
  between operations  14.2 us (8%)
  local copies, waits for them, and re-layouts  6.12 us (3%)
  other arithmetic  2.07 us (1%)
    ppermute x11, waiting for transfers between devices, shift_x(): return lax.ppermute(v, 'tp', pairs)  70.8 us
    pallas_call x3, Pallas kernels, project(): pl.pallas_call(functools.partial(project_kernel, plan_x, plan_w, len(xs),...  42.1 us
    ppermute x11, starting transfers between devices, shift_x(): return lax.ppermute(v, 'tp', pairs)  15.9 us
    ppermute x11, starting transfers between devices, swap_core(): return lax.ppermute(v, 'tp', [(t, t ^ 1) for t in range(2 * NX)])  12.1 us
    pallas_call x1, Pallas kernels, squares(): pl.pallas_call(squares_kernel, grid=(rows // tile,), out_shape=jax.ShapeD...  7.02 us
    ppermute x11, waiting for transfers between devices, swap_core(): return lax.ppermute(v, 'tp', [(t, t ^ 1) for t in range(2 * NX)])  6.22 us
  transfers between devices with their start and end apart: 23, of which 11 were waited for; matrix products, arithmetic and copies ran while one was open for 2% of the time, Pallas kernels for 21%

profile of v3, /device:TPU:1, one launch (start us, length us, event | category | flops | bytes accessed | tf_op | source)
XLA Modules:
  0.0 177.3 jit_solution(17752014505829426033)
XLA Ops:
  7.2 0.0 all-gather.2.cloned.1.call-start
  7.2 1.8 %pad_maximum_fusion = bf16[256,768]{1,0:T(8,128)(2,1)} fusion(bf16[256,128]{1,0:T(8,128)(2,1)} %param.17, bf16[256,128]{1,0:T(8,128)(2,1)} %param.16, bf16[256,512]{1,0:T(8,128)(2,1)} %param.15), kind=kLoop, calls=%fused_computation | loop fusion | flops 1179648 | bytes 786432 | tf_op jit(solution)/shard_map/concatenate | solution.py:283
  9.1 0.0 all-gather.2.cloned.1.call-update
  9.1 3.3 %collective-permute-start.3 = (bf16[1024,1024]{1,0:T(8,128)(2,1)}, bf16[1024,1024]{1,0:T(8,128)(2,1)}, u32[]{:S(2)}, u32[]{:S(2)}) collective-permute-start(bf16[1024,1024]{1,0:T(8,128)(2,1)} %refs_1_.2), channel_id=1, source_target_pairs={{0,1},{1,0},{2,3},{3,2},{4,5},{5,4},{6,7},{7,6},{8,9},{9,8},{10,11... | collective-permute-start | bytes 6291464 | tf_op jit(solution)/shard_map/ppermute | solution.py:25
  12.4 0.0 collective-permute-start
  12.4 2.7 %collective-permute-start.1 = (bf16[1024,512]{1,0:T(8,128)(2,1)}, bf16[1024,512]{1,0:T(8,128)(2,1)S(1)}, u32[]{:S(2)}, u32[]{:S(2)}) collective-permute-start(bf16[1024,512]{1,0:T(8,128)(2,1)} %refs_1_.1), channel_id=1, source_target_pairs={{0,6},{1,7},{2,0},{3,1},{4,2},{5,3},{6,4},{7,5},{8,14},{9,15},{10,... | collective-permute-start | bytes 3145736 | tf_op jit(solution)/shard_map/ppermute | solution.py:21
  15.1 0.6 collective-permute-start.2
  15.7 22.9 %collective-permute-done.refs_5_ = bf16[1024,512]{1,0:T(8,128)(2,1)S(1)} collective-permute-done((bf16[1024,512]{1,0:T(8,128)(2,1)}, bf16[1024,512]{1,0:T(8,128)(2,1)S(1)}, u32[]{:S(2)}, u32[]{:S(2)}) %collective-permute-start) | collective-permute-done | bytes 1048608 | tf_op jit(solution)/shard_map/ppermute | solution.py:21
  38.7 0.0 collective-permute-done.3.refs_1_.refs_2_
  38.7 0.1 collective-permute-start.4
  38.9 2.7 %collective-permute-start.5 = (bf16[512,512]{1,0:T(8,128)(2,1)S(1)}, bf16[512,512]{1,0:T(8,128)(2,1)}, u32[]{:S(2)}, u32[]{:S(2)}) collective-permute-start(bf16[512,512]{1,0:T(8,128)(2,1)S(1)} %slice.19), channel_id=1, source_target_pairs={{0,6},{1,7},{2,0},{3,1},{4,2},{5,3},{6,4},{7,5},{8,14},{9,15},{10,... | collective-permute-start | bytes 1572872 | tf_op jit(solution)/shard_map/ppermute | solution.py:21
  41.6 11.2 %collective-permute-done.4.refs_7_ = bf16[512,512]{1,0:T(8,128)(2,1)} collective-permute-done((bf16[512,512]{1,0:T(8,128)(2,1)S(1)}, bf16[512,512]{1,0:T(8,128)(2,1)}, u32[]{:S(2)}, u32[]{:S(2)}) %collective-permute-start.4) | collective-permute-done | bytes 524320 | tf_op jit(solution)/shard_map/ppermute | solution.py:21
  52.8 0.3 collective-permute-start.6
  53.1 2.4 %collective-permute-start.7 = (bf16[1024,1024]{1,0:T(8,128)(2,1)}, bf16[1024,1024]{1,0:T(8,128)(2,1)}, u32[]{:S(2)}, u32[]{:S(2)}) collective-permute-start(bf16[1024,1024]{1,0:T(8,128)(2,1)} %refs_1_.2), channel_id=1, source_target_pairs={{0,6},{1,7},{2,0},{3,1},{4,2},{5,3},{6,4},{7,5},{8,14},{9,15},{10,... | collective-permute-start | bytes 6291464 | tf_op jit(solution)/shard_map/ppermute | solution.py:21
  55.5 2.2 %collective-permute-start.8 = (bf16[1024,512]{1,0:T(8,128)(2,1)S(1)}, bf16[1024,512]{1,0:T(8,128)(2,1)S(1)}, u32[]{:S(2)}, u32[]{:S(2)}) collective-permute-start(bf16[1024,512]{1,0:T(8,128)(2,1)S(1)} %collective-permute-done.1.refs_3_), channel_id=1, source_target_pairs={{0,1},{1,0},{2,3},{3,2},{4,5},{5,4},{6,7},{7,6},{8,9},{9,8},{10,11... | collective-permute-start | bytes 3145736 | tf_op jit(solution)/shard_map/ppermute | solution.py:25
  57.7 0.5 collective-permute-start.10
  58.2 3.2 %collective-permute-done.8.refs_4_ = bf16[1024,512]{1,0:T(8,128)(2,1)S(1)} collective-permute-done((bf16[1024,512]{1,0:T(8,128)(2,1)S(1)}, bf16[1024,512]{1,0:T(8,128)(2,1)S(1)}, u32[]{:S(2)}, u32[]{:S(2)}) %collective-permute-start.8) | collective-permute-done | bytes 1048608 | tf_op jit(solution)/shard_map/ppermute | solution.py:25
  61.4 1.0 copy-done.5
  62.4 0.4 collective-permute-start.11
  62.8 0.1 pad_add_fusion.refs_0_
  62.9 0.1 broadcast_select_fusion.1.refs_15_
  63.0 1.7 collective-permute-done.11.refs_10_
  64.7 15.8 %shard_map.122.refs_10_ = f32[8,1024]{1,0:T(8,128)S(1)} custom-call(s32[2]{0:T(128)S(1)} %pad_add_fusion.refs_0_, bf16[1024,512]{1,0:T(8,128)(2,1)} %refs_1_.1, bf16[1024,512]{1,0:T(8,128)(2,1)} %collective-permute-done.2.refs_2_, bf16[1024,512]{1,0:T(8,128)(2,1)} %copy-done.4, bf16[1024,512]{1,0:T(8,128)(2,1)} %copy-done.5, bf16[1024,512]{1,0:T(8,128)(2,1)} %copy-done.3, ...), custom_call_target="tpu_custom_call" | custom-call | flops 1024 | bytes 1024 | tf_op jit(solution)/shard_map/pallas_call | solution.py:179
  80.4 19.4 %collective-permute-done.6.refs_4_.refs_5_ = bf16[1024,1024]{1,0:T(8,128)(2,1)S(1)} collective-permute-done((bf16[1024,1024]{1,0:T(8,128)(2,1)}, bf16[1024,1024]{1,0:T(8,128)(2,1)S(1)}, u32[]{:S(2)}, u32[]{:S(2)}) %collective-permute-start.6) | collective-permute-done | bytes 2097184 | tf_op jit(solution)/shard_map/ppermute | solution.py:21
  99.8 2.5 %collective-permute-start.14 = (bf16[1024,1024]{1,0:T(8,128)(2,1)}, bf16[1024,1024]{1,0:T(8,128)(2,1)}, u32[]{:S(2)}, u32[]{:S(2)}) collective-permute-start(bf16[1024,1024]{1,0:T(8,128)(2,1)} %collective-permute-done.7.refs_2_.refs_3_), channel_id=1, source_target_pairs={{0,1},{1,0},{2,3},{3,2},{4,5},{5,4},{6,7},{7,6},{8,9},{9,8},{10,11... | collective-permute-start | bytes 6291464 | tf_op jit(solution)/shard_map/ppermute | solution.py:25
  102.3 0.1 collective-permute-start.15
  102.4 1.1 slice.20
  103.5 2.3 %slice.21 = bf16[512,1024]{1,0:T(8,128)(2,1)} slice(bf16[1024,1024]{1,0:T(8,128)(2,1)} %collective-permute-done.7.refs_2_.refs_3_), slice={[512:1024], [0:1024]} | slice | bytes 2097152 | tf_op jit(solution)/shard_map/slice | solution.py:39
  105.8 0.7 collective-permute-start.12
  106.5 2.3 %collective-permute-start.13 = (bf16[512,1024]{1,0:T(8,128)(2,1)}, bf16[512,1024]{1,0:T(8,128)(2,1)}, u32[]{:S(2)}, u32[]{:S(2)}) collective-permute-start(bf16[512,1024]{1,0:T(8,128)(2,1)} %slice.21), channel_id=1, source_target_pairs={{0,6},{1,7},{2,0},{3,1},{4,2},{5,3},{6,4},{7,5},{8,14},{9,15},{10,... | collective-permute-start | bytes 3145736 | tf_op jit(solution)/shard_map/ppermute | solution.py:21
  108.8 0.4 collective-permute-done.15.refs_5_.refs_6_
  109.2 7.0 %shard_map.123.refs_6_ = f32[1024,128]{1,0:T(8,128)} custom-call(bf16[1024,1024]{1,0:T(8,128)(2,1)} %refs_1_.2, bf16[1024,1024]{1,0:T(8,128)(2,1)} %collective-permute-done.3.refs_1_.refs_2_, bf16[1024,1024]{1,0:T(8,128)(2,1)} %collective-permute-done.7.refs_2_.refs_3_, bf16[1024,1024]{1,0:T(8,128)(2,1)} %collective-permute-done.14.refs_3_.refs_4_, ...), custom_call_target="tpu_custom_call" | custom-call | flops 1024 | bytes 1024 | tf_op jit(solution)/shard_map/pallas_call | solution.py:252
  116.2 15.4 %collective-permute-done.12.refs_1_ = bf16[512,1024]{1,0:T(8,128)(2,1)S(1)} collective-permute-done((bf16[512,1024]{1,0:T(8,128)(2,1)}, bf16[512,1024]{1,0:T(8,128)(2,1)S(1)}, u32[]{:S(2)}, u32[]{:S(2)}) %collective-permute-start.12) | collective-permute-done | bytes 1048608 | tf_op jit(solution)/shard_map/ppermute | solution.py:21
  131.6 1.2 collective-permute-start.16
  132.9 0.1 collective-permute-start.17
  133.0 0.1 broadcast_select_fusion.refs_9_
  133.0 0.7 all-gather.2.cloned.1.call-done.refs_7_.refs_5_
  133.8 14.8 %shard_map.124.refs_7_ = f32[1024,768]{1,0:T(8,128)S(1)} custom-call(s32[2]{0:T(128)S(1)} %pad_add_fusion.refs_0_, bf16[1024,1024]{1,0:T(8,128)(2,1)} %refs_1_.2, bf16[1024,1024]{1,0:T(8,128)(2,1)} %collective-permute-done.3.refs_1_.refs_2_, bf16[1024,1024]{1,0:T(8,128)(2,1)} %collective-permute-done.7.refs_2_.refs_3_, ...), custom_call_target="tpu_custom_call" | custom-call | flops 1024 | bytes 1024 | tf_op jit(solution)/shard_map/pallas_call | solution.py:179
  148.6 1.0 copy-done.7
  149.6 11.6 %shard_map.125 = f32[8,1024]{1,0:T(8,128)S(1)} custom-call(s32[2]{0:T(128)S(1)} %pad_add_fusion.refs_0_, bf16[512,1024]{1,0:T(8,128)(2,1)} %copy-done.6, bf16[512,1024]{1,0:T(8,128)(2,1)} %copy-done.7, bf16[512,1024]{1,0:T(8,128)(2,1)} %collective-permute-done.13.refs_3_, bf16[512,1024]{1,0:T(8,128)(2,1)} %collective-permute-done.17.refs_4_, ...), custom_call_target="tpu_custom_call" | custom-call | flops 1024 | bytes 1024 | tf_op jit(solution)/shard_map/pallas_call | solution.py:179
  161.1 1.1 collective-permute-start.18
  162.3 0.9 collective-permute-done.18
  163.1 1.2 collective-permute-start.19
  164.3 2.4 %collective-permute-start.20 = (f32[8,1024]{1,0:T(8,128)S(1)}, f32[8,1024]{1,0:T(8,128)S(1)}, u32[]{:S(2)}, u32[]{:S(2)}) collective-permute-start(f32[8,1024]{1,0:T(8,128)S(1)} %add.18), channel_id=1, source_target_pairs={{0,4},{1,5},{2,6},{3,7},{4,0},{5,1},{6,2},{7,3},{8,12},{9,13},{10,... | collective-permute-start | bytes 98312 | tf_op jit(solution)/shard_map/ppermute | solution.py:21
  166.7 1.2 collective-permute-start.21
  167.9 0.8 collective-permute-done.20
  168.7 1.1 collective-permute-done.21
  169.8 0.6 fusion
  (37 shorter events, 0.2 us)
Async XLA Ops:
  7.2 55.7 %copy-start.8 = (bf16[512]{0:T(512)(128)(2,1)S(1)}, bf16[512]{0:T(512)(128)(2,1)}, u32[]{:S(2)}) copy-start(bf16[512]{0:T(512)(128)(2,1)} %param.22) | copy-start | bytes 3076
  7.2 57.5 %copy-start.1 = (s32[1024]{0:T(1024)S(1)}, s32[1024]{0:T(1024)}, u32[]{:S(2)}) copy-start(s32[1024]{0:T(1024)} %param.14) | copy-start | bytes 12292
  7.2 126.6 %all-gather.2.cloned.1.call-start = ((), (), s32[]{:S(2)}) async-start(), calls=%async_computation | async-start | bytes 12976128 | tf_op jit(solution)/shard_map/all_gather | solution.py:284
  9.1 29.6 %collective-permute-start.3 = (bf16[1024,1024]{1,0:T(8,128)(2,1)}, bf16[1024,1024]{1,0:T(8,128)(2,1)}, u32[]{:S(2)}, u32[]{:S(2)}) collective-permute-start(bf16[1024,1024]{1,0:T(8,128)(2,1)} %refs_1_.2), channel_id=1, source_target_pairs={{0,1},{1,0},{2,3},{3,2},{4,5},{5,4},{6,7},{7,6},{8,9},{9,8},{10,11... | collective-permute-start | bytes 6291464 | tf_op jit(solution)/shard_map/ppermute | solution.py:25
  12.4 26.2 %collective-permute-start = (bf16[1024,512]{1,0:T(8,128)(2,1)}, bf16[1024,512]{1,0:T(8,128)(2,1)S(1)}, u32[]{:S(2)}, u32[]{:S(2)}) collective-permute-start(bf16[1024,512]{1,0:T(8,128)(2,1)} %refs_1_.1), channel_id=1, source_target_pairs={{0,2},{1,3},{2,4},{3,5},{4,6},{5,7},{6,0},{7,1},{8,10},{9,11},{10,... | collective-permute-start | bytes 3145736 | tf_op jit(solution)/shard_map/ppermute | solution.py:21
  12.4 26.2 %collective-permute-start.1 = (bf16[1024,512]{1,0:T(8,128)(2,1)}, bf16[1024,512]{1,0:T(8,128)(2,1)S(1)}, u32[]{:S(2)}, u32[]{:S(2)}) collective-permute-start(bf16[1024,512]{1,0:T(8,128)(2,1)} %refs_1_.1), channel_id=1, source_target_pairs={{0,6},{1,7},{2,0},{3,1},{4,2},{5,3},{6,4},{7,5},{8,14},{9,15},{10,... | collective-permute-start | bytes 3145736 | tf_op jit(solution)/shard_map/ppermute | solution.py:21
  15.1 23.6 %collective-permute-start.2 = (bf16[1024,512]{1,0:T(8,128)(2,1)}, bf16[1024,512]{1,0:T(8,128)(2,1)}, u32[]{:S(2)}, u32[]{:S(2)}) collective-permute-start(bf16[1024,512]{1,0:T(8,128)(2,1)} %refs_1_.1), channel_id=1, source_target_pairs={{0,1},{1,0},{2,3},{3,2},{4,5},{5,4},{6,7},{7,6},{8,9},{9,8},{10,11... | collective-permute-start | bytes 3145736 | tf_op jit(solution)/shard_map/ppermute | solution.py:25
  38.6 26.0 %copy-start.3 = (bf16[1024,512]{1,0:T(8,128)(2,1)}, bf16[1024,512]{1,0:T(8,128)(2,1)S(1)}, u32[]{:S(2)}) copy-start(bf16[1024,512]{1,0:T(8,128)(2,1)S(1)} %collective-permute-done.refs_5_) | copy-start | bytes 3145732
  38.7 16.8 %copy-start.4 = (bf16[1024,512]{1,0:T(8,128)(2,1)}, bf16[1024,512]{1,0:T(8,128)(2,1)S(1)}, u32[]{:S(2)}) copy-start(bf16[1024,512]{1,0:T(8,128)(2,1)S(1)} %collective-permute-done.1.refs_3_) | copy-start | bytes 3145732
  38.7 14.1 %collective-permute-start.4 = (bf16[512,512]{1,0:T(8,128)(2,1)S(1)}, bf16[512,512]{1,0:T(8,128)(2,1)}, u32[]{:S(2)}, u32[]{:S(2)}) collective-permute-start(bf16[512,512]{1,0:T(8,128)(2,1)S(1)} %slice.18), channel_id=1, source_target_pairs={{0,2},{1,3},{2,4},{3,5},{4,6},{5,7},{6,0},{7,1},{8,10},{9,11},{10,... | collective-permute-start | bytes 1572872 | tf_op jit(solution)/shard_map/ppermute | solution.py:21
  38.9 13.9 %collective-permute-start.5 = (bf16[512,512]{1,0:T(8,128)(2,1)S(1)}, bf16[512,512]{1,0:T(8,128)(2,1)}, u32[]{:S(2)}, u32[]{:S(2)}) collective-permute-start(bf16[512,512]{1,0:T(8,128)(2,1)S(1)} %slice.19), channel_id=1, source_target_pairs={{0,6},{1,7},{2,0},{3,1},{4,2},{5,3},{6,4},{7,5},{8,14},{9,15},{10,... | collective-permute-start | bytes 1572872 | tf_op jit(solution)/shard_map/ppermute | solution.py:21
  52.8 47.0 %collective-permute-start.6 = (bf16[1024,1024]{1,0:T(8,128)(2,1)}, bf16[1024,1024]{1,0:T(8,128)(2,1)S(1)}, u32[]{:S(2)}, u32[]{:S(2)}) collective-permute-start(bf16[1024,1024]{1,0:T(8,128)(2,1)} %refs_1_.2), channel_id=1, source_target_pairs={{0,2},{1,3},{2,4},{3,5},{4,6},{5,7},{6,0},{7,1},{8,10},{9,11},{10,... | collective-permute-start | bytes 6291464 | tf_op jit(solution)/shard_map/ppermute | solution.py:21
  53.1 46.7 %collective-permute-start.7 = (bf16[1024,1024]{1,0:T(8,128)(2,1)}, bf16[1024,1024]{1,0:T(8,128)(2,1)}, u32[]{:S(2)}, u32[]{:S(2)}) collective-permute-start(bf16[1024,1024]{1,0:T(8,128)(2,1)} %refs_1_.2), channel_id=1, source_target_pairs={{0,6},{1,7},{2,0},{3,1},{4,2},{5,3},{6,4},{7,5},{8,14},{9,15},{10,... | collective-permute-start | bytes 6291464 | tf_op jit(solution)/shard_map/ppermute | solution.py:21
  55.5 6.0 %collective-permute-start.8 = (bf16[1024,512]{1,0:T(8,128)(2,1)S(1)}, bf16[1024,512]{1,0:T(8,128)(2,1)S(1)}, u32[]{:S(2)}, u32[]{:S(2)}) collective-permute-start(bf16[1024,512]{1,0:T(8,128)(2,1)S(1)} %collective-permute-done.1.refs_3_), channel_id=1, source_target_pairs={{0,1},{1,0},{2,3},{3,2},{4,5},{5,4},{6,7},{7,6},{8,9},{9,8},{10,11... | collective-permute-start | bytes 3145736 | tf_op jit(solution)/shard_map/ppermute | solution.py:25
  57.7 5.3 %collective-permute-start.9 = (bf16[1024,512]{1,0:T(8,128)(2,1)S(1)}, bf16[1024,512]{1,0:T(8,128)(2,1)}, u32[]{:S(2)}, u32[]{:S(2)}) collective-permute-start(bf16[1024,512]{1,0:T(8,128)(2,1)S(1)} %collective-permute-done.refs_5_), channel_id=1, source_target_pairs={{0,1},{1,0},{2,3},{3,2},{4,5},{5,4},{6,7},{7,6},{8,9},{9,8},{10,11... | collective-permute-start | bytes 3145736 | tf_op jit(solution)/shard_map/ppermute | solution.py:25
  57.7 5.3 %collective-permute-start.10 = (bf16[512,512]{1,0:T(8,128)(2,1)}, bf16[512,512]{1,0:T(8,128)(2,1)}, u32[]{:S(2)}, u32[]{:S(2)}) collective-permute-start(bf16[512,512]{1,0:T(8,128)(2,1)} %collective-permute-done.4.refs_7_), channel_id=1, source_target_pairs={{0,1},{1,0},{2,3},{3,2},{4,5},{5,4},{6,7},{7,6},{8,9},{9,8},{10,11... | collective-permute-start | bytes 1572872 | tf_op jit(solution)/shard_map/ppermute | solution.py:25
  61.4 1.0 copy-start.5
  62.4 2.3 %collective-permute-start.11 = (bf16[512,512]{1,0:T(8,128)(2,1)}, bf16[512,512]{1,0:T(8,128)(2,1)}, u32[]{:S(2)}, u32[]{:S(2)}) collective-permute-start(bf16[512,512]{1,0:T(8,128)(2,1)} %collective-permute-done.5.refs_9_), channel_id=1, source_target_pairs={{0,1},{1,0},{2,3},{3,2},{4,5},{5,4},{6,7},{7,6},{8,9},{9,8},{10,11... | collective-permute-start | bytes 1572872 | tf_op jit(solution)/shard_map/ppermute | solution.py:25
  99.8 6.0 %copy-start.2 = (bf16[1024,1024]{1,0:T(8,128)(2,1)}, bf16[1024,1024]{1,0:T(8,128)(2,1)S(1)}, u32[]{:S(2)}) copy-start(bf16[1024,1024]{1,0:T(8,128)(2,1)S(1)} %collective-permute-done.6.refs_4_.refs_5_) | copy-start | bytes 6291460
  99.8 9.0 %collective-permute-start.14 = (bf16[1024,1024]{1,0:T(8,128)(2,1)}, bf16[1024,1024]{1,0:T(8,128)(2,1)}, u32[]{:S(2)}, u32[]{:S(2)}) collective-permute-start(bf16[1024,1024]{1,0:T(8,128)(2,1)} %collective-permute-done.7.refs_2_.refs_3_), channel_id=1, source_target_pairs={{0,1},{1,0},{2,3},{3,2},{4,5},{5,4},{6,7},{7,6},{8,9},{9,8},{10,11... | collective-permute-start | bytes 6291464 | tf_op jit(solution)/shard_map/ppermute | solution.py:25
  102.3 6.9 %collective-permute-start.15 = (bf16[1024,1024]{1,0:T(8,128)(2,1)S(1)}, bf16[1024,1024]{1,0:T(8,128)(2,1)}, u32[]{:S(2)}, u32[]{:S(2)}) collective-permute-start(bf16[1024,1024]{1,0:T(8,128)(2,1)S(1)} %collective-permute-done.6.refs_4_.refs_5_), channel_id=1, source_target_pairs={{0,1},{1,0},{2,3},{3,2},{4,5},{5,4},{6,7},{7,6},{8,9},{9,8},{10,11... | collective-permute-start | bytes 6291464 | tf_op jit(solution)/shard_map/ppermute | solution.py:25
  105.8 27.1 %copy-start.9 = (bf16[512]{0:T(512)(128)(2,1)S(1)}, bf16[512]{0:T(512)(128)(2,1)}, u32[]{:S(2)}) copy-start(bf16[512]{0:T(512)(128)(2,1)} %param.21) | copy-start | bytes 3076
  105.8 25.8 %collective-permute-start.12 = (bf16[512,1024]{1,0:T(8,128)(2,1)}, bf16[512,1024]{1,0:T(8,128)(2,1)S(1)}, u32[]{:S(2)}, u32[]{:S(2)}) collective-permute-start(bf16[512,1024]{1,0:T(8,128)(2,1)} %slice.20), channel_id=1, source_target_pairs={{0,2},{1,3},{2,4},{3,5},{4,6},{5,7},{6,0},{7,1},{8,10},{9,11},{10,... | collective-permute-start | bytes 3145736 | tf_op jit(solution)/shard_map/ppermute | solution.py:21
  106.5 25.1 %collective-permute-start.13 = (bf16[512,1024]{1,0:T(8,128)(2,1)}, bf16[512,1024]{1,0:T(8,128)(2,1)}, u32[]{:S(2)}, u32[]{:S(2)}) collective-permute-start(bf16[512,1024]{1,0:T(8,128)(2,1)} %slice.21), channel_id=1, source_target_pairs={{0,6},{1,7},{2,0},{3,1},{4,2},{5,3},{6,4},{7,5},{8,14},{9,15},{10,... | collective-permute-start | bytes 3145736 | tf_op jit(solution)/shard_map/ppermute | solution.py:21
  131.6 16.9 %copy-start.6 = (bf16[512,1024]{1,0:T(8,128)(2,1)}, bf16[512,1024]{1,0:T(8,128)(2,1)S(1)}, u32[]{:S(2)}) copy-start(bf16[512,1024]{1,0:T(8,128)(2,1)S(1)} %collective-permute-done.12.refs_1_) | copy-start | bytes 3145732
  131.6 16.9 %collective-permute-start.16 = (bf16[512,1024]{1,0:T(8,128)(2,1)S(1)}, bf16[512,1024]{1,0:T(8,128)(2,1)S(1)}, u32[]{:S(2)}, u32[]{:S(2)}) collective-permute-start(bf16[512,1024]{1,0:T(8,128)(2,1)S(1)} %collective-permute-done.12.refs_1_), channel_id=1, source_target_pairs={{0,1},{1,0},{2,3},{3,2},{4,5},{5,4},{6,7},{7,6},{8,9},{9,8},{10,11... | collective-permute-start | bytes 3145736 | tf_op jit(solution)/shard_map/ppermute | solution.py:25
  132.9 15.7 %collective-permute-start.17 = (bf16[512,1024]{1,0:T(8,128)(2,1)}, bf16[512,1024]{1,0:T(8,128)(2,1)}, u32[]{:S(2)}, u32[]{:S(2)}) collective-permute-start(bf16[512,1024]{1,0:T(8,128)(2,1)} %collective-permute-done.13.refs_3_), channel_id=1, source_target_pairs={{0,1},{1,0},{2,3},{3,2},{4,5},{5,4},{6,7},{7,6},{8,9},{9,8},{10,11... | collective-permute-start | bytes 3145736 | tf_op jit(solution)/shard_map/ppermute | solution.py:25
  133.0 16.5 %copy-start = (f32[1024,128]{1,0:T(8,128)S(1)}, f32[1024,128]{1,0:T(8,128)}, u32[]{:S(2)}) copy-start(f32[1024,128]{1,0:T(8,128)} %shard_map.123.refs_6_) | copy-start | bytes 1572868
  148.6 1.0 copy-start.7
  161.1 2.0 %collective-permute-start.18 = (f32[8,1024]{1,0:T(8,128)S(1)}, f32[8,1024]{1,0:T(8,128)S(1)}, u32[]{:S(2)}, u32[]{:S(2)}) collective-permute-start(f32[8,1024]{1,0:T(8,128)S(1)} %shard_map.125), channel_id=1, source_target_pairs={{0,1},{1,0},{2,3},{3,2},{4,5},{5,4},{6,7},{7,6},{8,9},{9,8},{10,11... | collective-permute-start | bytes 98312 | tf_op jit(solution)/shard_map/ppermute | solution.py:25
  163.1 4.8 %collective-permute-start.19 = (f32[8,1024]{1,0:T(8,128)S(1)}, f32[8,1024]{1,0:T(8,128)S(1)}, u32[]{:S(2)}, u32[]{:S(2)}) collective-permute-start(f32[8,1024]{1,0:T(8,128)S(1)} %add.18), channel_id=1, source_target_pairs={{0,2},{1,3},{2,4},{3,5},{4,6},{5,7},{6,0},{7,1},{8,10},{9,11},{10,... | collective-permute-start | bytes 98312 | tf_op jit(solution)/shard_map/ppermute | solution.py:21
  164.3 4.4 %collective-permute-start.20 = (f32[8,1024]{1,0:T(8,128)S(1)}, f32[8,1024]{1,0:T(8,128)S(1)}, u32[]{:S(2)}, u32[]{:S(2)}) collective-permute-start(f32[8,1024]{1,0:T(8,128)S(1)} %add.18), channel_id=1, source_target_pairs={{0,4},{1,5},{2,6},{3,7},{4,0},{5,1},{6,2},{7,3},{8,12},{9,13},{10,... | collective-permute-start | bytes 98312 | tf_op jit(solution)/shard_map/ppermute | solution.py:21
  166.7 3.1 %collective-permute-start.21 = (f32[8,1024]{1,0:T(8,128)S(1)}, f32[8,1024]{1,0:T(8,128)S(1)}, u32[]{:S(2)}, u32[]{:S(2)}) collective-permute-start(f32[8,1024]{1,0:T(8,128)S(1)} %add.18), channel_id=1, source_target_pairs={{0,6},{1,7},{2,0},{3,1},{4,2},{5,3},{6,4},{7,5},{8,14},{9,15},{10,... | collective-permute-start | bytes 98312 | tf_op jit(solution)/shard_map/ppermute | solution.py:21
Sparse Core Ops, SparseCore 0:
  10.6 123.1 all-gather.1

commit v4 on v3

--- a/solution.py
+++ b/solution.py
@@ -52,10 +52,10 @@
     jds = lax.broadcasted_iota(jnp.int32, (tile, tile), 0)
     ids = lax.broadcasted_iota(jnp.int32, (tile, tile), 1)
 
-    @pl.loop(0, acc.shape[0] // tile // 2)
-    def _(pair):
-        for u in range(2):
-            at = pl.ds(aligned((pair * 2 + u) * tile, tile), tile)
+    @pl.loop(0, acc.shape[0] // tile // 4)
+    def _(four):
+        for u in range(4):
+            at = pl.ds(aligned((four * 4 + u) * tile, tile), tile)
             part = acc[at, :].astype(BF)
             queries = jnp.concatenate([part[:, h * HD : (h + 1) * HD] for h in range(4)], axis=0)
             keys, values = part[:, 4 * HD : 5 * HD], part[:, 5 * HD :]
@@ -137,9 +137,9 @@
 
         pltpu.make_async_copy(wbuf.at[s], wbuf.at[s], sems.at[1, s]).wait()
 
-        @pl.loop(0, rows // 512)
+        @pl.loop(0, rows // 1024)
         def _(m):
-            at = pl.ds(aligned(m * 512, 512), 512)
+            at = pl.ds(aligned(m * 1024, 1024), 1024)
             for k in range(0, width, 1024):
                 acc[at, :] += jnp.dot(
                     xbuf[s, at, k : k + 1024], wbuf[s, k : k + 1024, :], preferred_element_type=F32
@@ -233,6 +233,18 @@
     return [(which, place)]
 
 
+def whole_plan(which, rows):
+    return [(which, lambda pos: (None, [((EVERY, EVERY), (pl.ds(*rows), EVERY))]))]
+
+
+def side_weights(which, ahead, other):
+    def place(pos):
+        first = origin(pos, ahead) * 2048 + side(pos, other) * 1024
+        return None, [((pl.ds(aligned(first, 1024), 1024), EVERY), (EVERY, EVERY))]
+
+    return [(which, place)]
+
+
 def squares_kernel(*refs):
     xs, out_ref = refs[:-1], refs[-1]
 
@@ -332,18 +344,18 @@
         slots,
     )
     far, total = lax.optimization_barrier((far, total))
-    far_x, plan_x = [], [[]]
+    far_x, plan_x = [], [[], []]
     for index, v in enumerate(far):
         far_x += [v, swap_core(v)]
         for other in range(2):
-            plan_x[0] += ref_rows_plan(2 * index + other, other == 1, (index * half, half))
+            plan_x[other] += whole_plan(2 * index + other, (index * half, half))
     partial = project(
         pos,
         far_x,
         [gathered],
         plan_x,
-        [gathered_weights(0, 2)],
-        2048,
+        [side_weights(0, 2, other == 1) for other in range(2)],
+        1024,
         slots,
         prior=(total, near),
         finish=(0, 8192, seg_row, ref_readout, critic_part),

time: 178 us -> 176 us (0.989)
  Pallas kernels: 49.1 us -> 46.6 us
    pallas_call x3, Pallas kernels: 42.1 us -> 39.6 us  [project(): pl.pallas_call(functools.partial(project_kernel, plan_x, plan_w, len(xs),...]
  transfers between devices with their start and end apart: 23 -> 23, of which waited for: 11 -> 11; matrix products, arithmetic and copies ran while one was open for 2% -> 2% of each run, Pallas kernels for 21% -> 20%
where the time goes in v4:
time: 176 us
  waiting for transfers between devices  79.3 us (45%)
  Pallas kernels  46.6 us (26%)
  starting transfers between devices  27.7 us (16%)
  between operations  14.2 us (8%)
  local copies, waits for them, and re-layouts  6.13 us (3%)
  other arithmetic  2.07 us (1%)
    ppermute x11, waiting for transfers between devices, shift_x(): return lax.ppermute(v, 'tp', pairs)  72.4 us
    pallas_call x3, Pallas kernels, project(): pl.pallas_call(functools.partial(project_kernel, plan_x, plan_w, len(xs),...  39.6 us
    ppermute x11, starting transfers between devices, shift_x(): return lax.ppermute(v, 'tp', pairs)  15.6 us
    ppermute x11, starting transfers between devices, swap_core(): return lax.ppermute(v, 'tp', [(t, t ^ 1) for t in range(2 * NX)])  12.1 us
    pallas_call x1, Pallas kernels, squares(): pl.pallas_call(squares_kernel, grid=(rows // tile,), out_shape=jax.ShapeD...  7.02 us
    ppermute x11, waiting for transfers between devices, swap_core(): return lax.ppermute(v, 'tp', [(t, t ^ 1) for t in range(2 * NX)])  6.33 us
    slice x4, local copies, waits for them, and re-layouts, step_two(): return (shift_x(before[:half], 1), shift_x(after[half:], -1))  3.54 us
  transfers between devices with their start and end apart: 23, of which 11 were waited for; matrix products, arithmetic and copies ran while one was open for 2% of the time, Pallas kernels for 20%

profile of v4, /device:TPU:1, one launch (start us, length us, event | category | flops | bytes accessed | tf_op | source)
XLA Modules:
  0.0 176.0 jit_solution(7239577266070421699)
XLA Ops:
  7.2 0.0 all-gather.2.cloned.1.call-start
  7.2 1.8 %pad_maximum_fusion = bf16[256,768]{1,0:T(8,128)(2,1)} fusion(bf16[256,128]{1,0:T(8,128)(2,1)} %param.17, bf16[256,128]{1,0:T(8,128)(2,1)} %param.16, bf16[256,512]{1,0:T(8,128)(2,1)} %param.15), kind=kLoop, calls=%fused_computation | loop fusion | flops 1179648 | bytes 786432 | tf_op jit(solution)/shard_map/concatenate | solution.py:295
  9.1 0.0 all-gather.2.cloned.1.call-update
  9.1 3.3 %collective-permute-start.3 = (bf16[1024,1024]{1,0:T(8,128)(2,1)}, bf16[1024,1024]{1,0:T(8,128)(2,1)}, u32[]{:S(2)}, u32[]{:S(2)}) collective-permute-start(bf16[1024,1024]{1,0:T(8,128)(2,1)} %refs_1_.2), channel_id=1, source_target_pairs={{0,1},{1,0},{2,3},{3,2},{4,5},{5,4},{6,7},{7,6},{8,9},{9,8},{10,11... | collective-permute-start | bytes 6291464 | tf_op jit(solution)/shard_map/ppermute | solution.py:25
  12.4 2.7 %collective-permute-start.1 = (bf16[1024,512]{1,0:T(8,128)(2,1)}, bf16[1024,512]{1,0:T(8,128)(2,1)S(1)}, u32[]{:S(2)}, u32[]{:S(2)}) collective-permute-start(bf16[1024,512]{1,0:T(8,128)(2,1)} %refs_1_.1), channel_id=1, source_target_pairs={{0,6},{1,7},{2,0},{3,1},{4,2},{5,3},{6,4},{7,5},{8,14},{9,15},{10,... | collective-permute-start | bytes 3145736 | tf_op jit(solution)/shard_map/ppermute | solution.py:21
  15.1 0.6 collective-permute-start.2
  15.7 22.9 %collective-permute-done.refs_5_ = bf16[1024,512]{1,0:T(8,128)(2,1)S(1)} collective-permute-done((bf16[1024,512]{1,0:T(8,128)(2,1)}, bf16[1024,512]{1,0:T(8,128)(2,1)S(1)}, u32[]{:S(2)}, u32[]{:S(2)}) %collective-permute-start) | collective-permute-done | bytes 1048608 | tf_op jit(solution)/shard_map/ppermute | solution.py:21
  38.6 0.0 collective-permute-done.1.refs_3_
  38.7 0.0 collective-permute-done.2.refs_2_
  38.7 0.1 collective-permute-start.4
  38.9 2.7 %collective-permute-start.5 = (bf16[512,512]{1,0:T(8,128)(2,1)S(1)}, bf16[512,512]{1,0:T(8,128)(2,1)}, u32[]{:S(2)}, u32[]{:S(2)}) collective-permute-start(bf16[512,512]{1,0:T(8,128)(2,1)S(1)} %slice.19), channel_id=1, source_target_pairs={{0,6},{1,7},{2,0},{3,1},{4,2},{5,3},{6,4},{7,5},{8,14},{9,15},{10,... | collective-permute-start | bytes 1572872 | tf_op jit(solution)/shard_map/ppermute | solution.py:21
  41.6 11.2 %collective-permute-done.4.refs_7_ = bf16[512,512]{1,0:T(8,128)(2,1)} collective-permute-done((bf16[512,512]{1,0:T(8,128)(2,1)S(1)}, bf16[512,512]{1,0:T(8,128)(2,1)}, u32[]{:S(2)}, u32[]{:S(2)}) %collective-permute-start.4) | collective-permute-done | bytes 524320 | tf_op jit(solution)/shard_map/ppermute | solution.py:21
  52.8 0.3 collective-permute-start.6
  53.1 2.4 %collective-permute-start.7 = (bf16[1024,1024]{1,0:T(8,128)(2,1)}, bf16[1024,1024]{1,0:T(8,128)(2,1)}, u32[]{:S(2)}, u32[]{:S(2)}) collective-permute-start(bf16[1024,1024]{1,0:T(8,128)(2,1)} %refs_1_.2), channel_id=1, source_target_pairs={{0,6},{1,7},{2,0},{3,1},{4,2},{5,3},{6,4},{7,5},{8,14},{9,15},{10,... | collective-permute-start | bytes 6291464 | tf_op jit(solution)/shard_map/ppermute | solution.py:21
  55.5 2.2 %collective-permute-start.8 = (bf16[1024,512]{1,0:T(8,128)(2,1)S(1)}, bf16[1024,512]{1,0:T(8,128)(2,1)S(1)}, u32[]{:S(2)}, u32[]{:S(2)}) collective-permute-start(bf16[1024,512]{1,0:T(8,128)(2,1)S(1)} %collective-permute-done.1.refs_3_), channel_id=1, source_target_pairs={{0,1},{1,0},{2,3},{3,2},{4,5},{5,4},{6,7},{7,6},{8,9},{9,8},{10,11... | collective-permute-start | bytes 3145736 | tf_op jit(solution)/shard_map/ppermute | solution.py:25
  57.7 0.5 collective-permute-start.10
  58.2 3.2 %collective-permute-done.8.refs_4_ = bf16[1024,512]{1,0:T(8,128)(2,1)S(1)} collective-permute-done((bf16[1024,512]{1,0:T(8,128)(2,1)S(1)}, bf16[1024,512]{1,0:T(8,128)(2,1)S(1)}, u32[]{:S(2)}, u32[]{:S(2)}) %collective-permute-start.8) | collective-permute-done | bytes 1048608 | tf_op jit(solution)/shard_map/ppermute | solution.py:25
  61.4 1.0 copy-done.5
  62.4 0.4 collective-permute-start.11
  62.8 0.1 pad_add_fusion.refs_0_
  62.9 0.1 broadcast_select_fusion.1.refs_15_
  63.0 1.7 collective-permute-done.11.refs_10_
  64.7 14.5 %shard_map.122.refs_10_ = f32[8,1024]{1,0:T(8,128)S(1)} custom-call(s32[2]{0:T(128)S(1)} %pad_add_fusion.refs_0_, bf16[1024,512]{1,0:T(8,128)(2,1)} %refs_1_.1, bf16[1024,512]{1,0:T(8,128)(2,1)} %collective-permute-done.2.refs_2_, bf16[1024,512]{1,0:T(8,128)(2,1)} %copy-done.4, bf16[1024,512]{1,0:T(8,128)(2,1)} %copy-done.5, bf16[1024,512]{1,0:T(8,128)(2,1)} %copy-done.3, ...), custom_call_target="tpu_custom_call" | custom-call | flops 1024 | bytes 1024 | tf_op jit(solution)/shard_map/pallas_call | solution.py:179
  79.2 20.6 %collective-permute-done.6.refs_4_.refs_5_ = bf16[1024,1024]{1,0:T(8,128)(2,1)S(1)} collective-permute-done((bf16[1024,1024]{1,0:T(8,128)(2,1)}, bf16[1024,1024]{1,0:T(8,128)(2,1)S(1)}, u32[]{:S(2)}, u32[]{:S(2)}) %collective-permute-start.6) | collective-permute-done | bytes 2097184 | tf_op jit(solution)/shard_map/ppermute | solution.py:21
  99.8 2.5 %collective-permute-start.14 = (bf16[1024,1024]{1,0:T(8,128)(2,1)}, bf16[1024,1024]{1,0:T(8,128)(2,1)}, u32[]{:S(2)}, u32[]{:S(2)}) collective-permute-start(bf16[1024,1024]{1,0:T(8,128)(2,1)} %collective-permute-done.7.refs_2_.refs_3_), channel_id=1, source_target_pairs={{0,1},{1,0},{2,3},{3,2},{4,5},{5,4},{6,7},{7,6},{8,9},{9,8},{10,11... | collective-permute-start | bytes 6291464 | tf_op jit(solution)/shard_map/ppermute | solution.py:25
  102.3 0.3 collective-permute-start.15
  102.5 1.1 slice.20
  103.7 2.3 %slice.21 = bf16[512,1024]{1,0:T(8,128)(2,1)} slice(bf16[1024,1024]{1,0:T(8,128)(2,1)} %collective-permute-done.7.refs_2_.refs_3_), slice={[512:1024], [0:1024]} | slice | bytes 2097152 | tf_op jit(solution)/shard_map/slice | solution.py:39
  106.0 0.5 collective-permute-start.12
  106.5 2.2 %collective-permute-start.13 = (bf16[512,1024]{1,0:T(8,128)(2,1)}, bf16[512,1024]{1,0:T(8,128)(2,1)}, u32[]{:S(2)}, u32[]{:S(2)}) collective-permute-start(bf16[512,1024]{1,0:T(8,128)(2,1)} %slice.21), channel_id=1, source_target_pairs={{0,6},{1,7},{2,0},{3,1},{4,2},{5,3},{6,4},{7,5},{8,14},{9,15},{10,... | collective-permute-start | bytes 3145736 | tf_op jit(solution)/shard_map/ppermute | solution.py:21
  108.7 0.5 collective-permute-done.15.refs_5_.refs_6_
  109.2 7.0 %shard_map.123.refs_6_ = f32[1024,128]{1,0:T(8,128)} custom-call(bf16[1024,1024]{1,0:T(8,128)(2,1)} %refs_1_.2, bf16[1024,1024]{1,0:T(8,128)(2,1)} %collective-permute-done.3.refs_1_.refs_2_, bf16[1024,1024]{1,0:T(8,128)(2,1)} %collective-permute-done.7.refs_2_.refs_3_, bf16[1024,1024]{1,0:T(8,128)(2,1)} %collective-permute-done.14.refs_3_.refs_4_, ...), custom_call_target="tpu_custom_call" | custom-call | flops 1024 | bytes 1024 | tf_op jit(solution)/shard_map/pallas_call | solution.py:264
  116.2 15.8 %collective-permute-done.12.refs_1_ = bf16[512,1024]{1,0:T(8,128)(2,1)S(1)} collective-permute-done((bf16[512,1024]{1,0:T(8,128)(2,1)}, bf16[512,1024]{1,0:T(8,128)(2,1)S(1)}, u32[]{:S(2)}, u32[]{:S(2)}) %collective-permute-start.12) | collective-permute-done | bytes 1048608 | tf_op jit(solution)/shard_map/ppermute | solution.py:21
  132.0 1.0 collective-permute-start.16
  133.0 0.1 collective-permute-start.17
  133.1 0.1 broadcast_select_fusion.refs_9_
  133.2 0.6 all-gather.2.cloned.1.call-done.refs_7_.refs_5_
  133.8 14.3 %shard_map.124.refs_7_ = f32[1024,768]{1,0:T(8,128)S(1)} custom-call(s32[2]{0:T(128)S(1)} %pad_add_fusion.refs_0_, bf16[1024,1024]{1,0:T(8,128)(2,1)} %refs_1_.2, bf16[1024,1024]{1,0:T(8,128)(2,1)} %collective-permute-done.3.refs_1_.refs_2_, bf16[1024,1024]{1,0:T(8,128)(2,1)} %collective-permute-done.7.refs_2_.refs_3_, ...), custom_call_target="tpu_custom_call" | custom-call | flops 1024 | bytes 1024 | tf_op jit(solution)/shard_map/pallas_call | solution.py:179
  148.1 1.0 copy-done.7
  149.1 10.7 %shard_map.125 = f32[8,1024]{1,0:T(8,128)S(1)} custom-call(s32[2]{0:T(128)S(1)} %pad_add_fusion.refs_0_, bf16[512,1024]{1,0:T(8,128)(2,1)} %copy-done.6, bf16[512,1024]{1,0:T(8,128)(2,1)} %copy-done.7, bf16[512,1024]{1,0:T(8,128)(2,1)} %collective-permute-done.13.refs_3_, bf16[512,1024]{1,0:T(8,128)(2,1)} %collective-permute-done.17.refs_4_, ...), custom_call_target="tpu_custom_call" | custom-call | flops 1024 | bytes 1024 | tf_op jit(solution)/shard_map/pallas_call | solution.py:179
  159.9 1.1 collective-permute-start.18
  161.0 0.9 collective-permute-done.18
  161.9 1.2 collective-permute-start.19
  163.1 2.4 %collective-permute-start.20 = (f32[8,1024]{1,0:T(8,128)S(1)}, f32[8,1024]{1,0:T(8,128)S(1)}, u32[]{:S(2)}, u32[]{:S(2)}) collective-permute-start(f32[8,1024]{1,0:T(8,128)S(1)} %add.18), channel_id=1, source_target_pairs={{0,4},{1,5},{2,6},{3,7},{4,0},{5,1},{6,2},{7,3},{8,12},{9,13},{10,... | collective-permute-start | bytes 98312 | tf_op jit(solution)/shard_map/ppermute | solution.py:21
  165.5 1.2 collective-permute-start.21
  166.7 0.8 collective-permute-done.20
  167.4 1.1 collective-permute-done.21
  168.5 0.6 fusion
  (37 shorter events, 0.2 us)
Async XLA Ops:
  7.2 55.7 %copy-start.8 = (bf16[512]{0:T(512)(128)(2,1)S(1)}, bf16[512]{0:T(512)(128)(2,1)}, u32[]{:S(2)}) copy-start(bf16[512]{0:T(512)(128)(2,1)} %param.22) | copy-start | bytes 3076
  7.2 57.5 %copy-start.1 = (s32[1024]{0:T(1024)S(1)}, s32[1024]{0:T(1024)}, u32[]{:S(2)}) copy-start(s32[1024]{0:T(1024)} %param.14) | copy-start | bytes 12292
  7.2 126.6 %all-gather.2.cloned.1.call-start = ((), (), s32[]{:S(2)}) async-start(), calls=%async_computation | async-start | bytes 12976128 | tf_op jit(solution)/shard_map/all_gather | solution.py:296
  9.1 29.6 %collective-permute-start.3 = (bf16[1024,1024]{1,0:T(8,128)(2,1)}, bf16[1024,1024]{1,0:T(8,128)(2,1)}, u32[]{:S(2)}, u32[]{:S(2)}) collective-permute-start(bf16[1024,1024]{1,0:T(8,128)(2,1)} %refs_1_.2), channel_id=1, source_target_pairs={{0,1},{1,0},{2,3},{3,2},{4,5},{5,4},{6,7},{7,6},{8,9},{9,8},{10,11... | collective-permute-start | bytes 6291464 | tf_op jit(solution)/shard_map/ppermute | solution.py:25
  12.4 26.2 %collective-permute-start = (bf16[1024,512]{1,0:T(8,128)(2,1)}, bf16[1024,512]{1,0:T(8,128)(2,1)S(1)}, u32[]{:S(2)}, u32[]{:S(2)}) collective-permute-start(bf16[1024,512]{1,0:T(8,128)(2,1)} %refs_1_.1), channel_id=1, source_target_pairs={{0,2},{1,3},{2,4},{3,5},{4,6},{5,7},{6,0},{7,1},{8,10},{9,11},{10,... | collective-permute-start | bytes 3145736 | tf_op jit(solution)/shard_map/ppermute | solution.py:21
  12.4 26.2 %collective-permute-start.1 = (bf16[1024,512]{1,0:T(8,128)(2,1)}, bf16[1024,512]{1,0:T(8,128)(2,1)S(1)}, u32[]{:S(2)}, u32[]{:S(2)}) collective-permute-start(bf16[1024,512]{1,0:T(8,128)(2,1)} %refs_1_.1), channel_id=1, source_target_pairs={{0,6},{1,7},{2,0},{3,1},{4,2},{5,3},{6,4},{7,5},{8,14},{9,15},{10,... | collective-permute-start | bytes 3145736 | tf_op jit(solution)/shard_map/ppermute | solution.py:21
  15.1 23.6 %collective-permute-start.2 = (bf16[1024,512]{1,0:T(8,128)(2,1)}, bf16[1024,512]{1,0:T(8,128)(2,1)}, u32[]{:S(2)}, u32[]{:S(2)}) collective-permute-start(bf16[1024,512]{1,0:T(8,128)(2,1)} %refs_1_.1), channel_id=1, source_target_pairs={{0,1},{1,0},{2,3},{3,2},{4,5},{5,4},{6,7},{7,6},{8,9},{9,8},{10,11... | collective-permute-start | bytes 3145736 | tf_op jit(solution)/shard_map/ppermute | solution.py:25
  38.6 26.0 %copy-start.3 = (bf16[1024,512]{1,0:T(8,128)(2,1)}, bf16[1024,512]{1,0:T(8,128)(2,1)S(1)}, u32[]{:S(2)}) copy-start(bf16[1024,512]{1,0:T(8,128)(2,1)S(1)} %collective-permute-done.refs_5_) | copy-start | bytes 3145732
  38.7 16.8 %copy-start.4 = (bf16[1024,512]{1,0:T(8,128)(2,1)}, bf16[1024,512]{1,0:T(8,128)(2,1)S(1)}, u32[]{:S(2)}) copy-start(bf16[1024,512]{1,0:T(8,128)(2,1)S(1)} %collective-permute-done.1.refs_3_) | copy-start | bytes 3145732
  38.7 14.1 %collective-permute-start.4 = (bf16[512,512]{1,0:T(8,128)(2,1)S(1)}, bf16[512,512]{1,0:T(8,128)(2,1)}, u32[]{:S(2)}, u32[]{:S(2)}) collective-permute-start(bf16[512,512]{1,0:T(8,128)(2,1)S(1)} %slice.18), channel_id=1, source_target_pairs={{0,2},{1,3},{2,4},{3,5},{4,6},{5,7},{6,0},{7,1},{8,10},{9,11},{10,... | collective-permute-start | bytes 1572872 | tf_op jit(solution)/shard_map/ppermute | solution.py:21
  38.9 13.9 %collective-permute-start.5 = (bf16[512,512]{1,0:T(8,128)(2,1)S(1)}, bf16[512,512]{1,0:T(8,128)(2,1)}, u32[]{:S(2)}, u32[]{:S(2)}) collective-permute-start(bf16[512,512]{1,0:T(8,128)(2,1)S(1)} %slice.19), channel_id=1, source_target_pairs={{0,6},{1,7},{2,0},{3,1},{4,2},{5,3},{6,4},{7,5},{8,14},{9,15},{10,... | collective-permute-start | bytes 1572872 | tf_op jit(solution)/shard_map/ppermute | solution.py:21
  52.8 47.0 %collective-permute-start.6 = (bf16[1024,1024]{1,0:T(8,128)(2,1)}, bf16[1024,1024]{1,0:T(8,128)(2,1)S(1)}, u32[]{:S(2)}, u32[]{:S(2)}) collective-permute-start(bf16[1024,1024]{1,0:T(8,128)(2,1)} %refs_1_.2), channel_id=1, source_target_pairs={{0,2},{1,3},{2,4},{3,5},{4,6},{5,7},{6,0},{7,1},{8,10},{9,11},{10,... | collective-permute-start | bytes 6291464 | tf_op jit(solution)/shard_map/ppermute | solution.py:21
  53.1 46.7 %collective-permute-start.7 = (bf16[1024,1024]{1,0:T(8,128)(2,1)}, bf16[1024,1024]{1,0:T(8,128)(2,1)}, u32[]{:S(2)}, u32[]{:S(2)}) collective-permute-start(bf16[1024,1024]{1,0:T(8,128)(2,1)} %refs_1_.2), channel_id=1, source_target_pairs={{0,6},{1,7},{2,0},{3,1},{4,2},{5,3},{6,4},{7,5},{8,14},{9,15},{10,... | collective-permute-start | bytes 6291464 | tf_op jit(solution)/shard_map/ppermute | solution.py:21
  55.5 6.0 %collective-permute-start.8 = (bf16[1024,512]{1,0:T(8,128)(2,1)S(1)}, bf16[1024,512]{1,0:T(8,128)(2,1)S(1)}, u32[]{:S(2)}, u32[]{:S(2)}) collective-permute-start(bf16[1024,512]{1,0:T(8,128)(2,1)S(1)} %collective-permute-done.1.refs_3_), channel_id=1, source_target_pairs={{0,1},{1,0},{2,3},{3,2},{4,5},{5,4},{6,7},{7,6},{8,9},{9,8},{10,11... | collective-permute-start | bytes 3145736 | tf_op jit(solution)/shard_map/ppermute | solution.py:25
  57.7 5.3 %collective-permute-start.9 = (bf16[1024,512]{1,0:T(8,128)(2,1)S(1)}, bf16[1024,512]{1,0:T(8,128)(2,1)}, u32[]{:S(2)}, u32[]{:S(2)}) collective-permute-start(bf16[1024,512]{1,0:T(8,128)(2,1)S(1)} %collective-permute-done.refs_5_), channel_id=1, source_target_pairs={{0,1},{1,0},{2,3},{3,2},{4,5},{5,4},{6,7},{7,6},{8,9},{9,8},{10,11... | collective-permute-start | bytes 3145736 | tf_op jit(solution)/shard_map/ppermute | solution.py:25
  57.7 5.3 %collective-permute-start.10 = (bf16[512,512]{1,0:T(8,128)(2,1)}, bf16[512,512]{1,0:T(8,128)(2,1)}, u32[]{:S(2)}, u32[]{:S(2)}) collective-permute-start(bf16[512,512]{1,0:T(8,128)(2,1)} %collective-permute-done.4.refs_7_), channel_id=1, source_target_pairs={{0,1},{1,0},{2,3},{3,2},{4,5},{5,4},{6,7},{7,6},{8,9},{9,8},{10,11... | collective-permute-start | bytes 1572872 | tf_op jit(solution)/shard_map/ppermute | solution.py:25
  61.4 1.0 copy-start.5
  62.4 2.3 %collective-permute-start.11 = (bf16[512,512]{1,0:T(8,128)(2,1)}, bf16[512,512]{1,0:T(8,128)(2,1)}, u32[]{:S(2)}, u32[]{:S(2)}) collective-permute-start(bf16[512,512]{1,0:T(8,128)(2,1)} %collective-permute-done.5.refs_9_), channel_id=1, source_target_pairs={{0,1},{1,0},{2,3},{3,2},{4,5},{5,4},{6,7},{7,6},{8,9},{9,8},{10,11... | collective-permute-start | bytes 1572872 | tf_op jit(solution)/shard_map/ppermute | solution.py:25
  99.8 6.2 %copy-start.2 = (bf16[1024,1024]{1,0:T(8,128)(2,1)}, bf16[1024,1024]{1,0:T(8,128)(2,1)S(1)}, u32[]{:S(2)}) copy-start(bf16[1024,1024]{1,0:T(8,128)(2,1)S(1)} %collective-permute-done.6.refs_4_.refs_5_) | copy-start | bytes 6291460
  99.8 8.9 %collective-permute-start.14 = (bf16[1024,1024]{1,0:T(8,128)(2,1)}, bf16[1024,1024]{1,0:T(8,128)(2,1)}, u32[]{:S(2)}, u32[]{:S(2)}) collective-permute-start(bf16[1024,1024]{1,0:T(8,128)(2,1)} %collective-permute-done.7.refs_2_.refs_3_), channel_id=1, source_target_pairs={{0,1},{1,0},{2,3},{3,2},{4,5},{5,4},{6,7},{7,6},{8,9},{9,8},{10,11... | collective-permute-start | bytes 6291464 | tf_op jit(solution)/shard_map/ppermute | solution.py:25
  102.3 6.9 %collective-permute-start.15 = (bf16[1024,1024]{1,0:T(8,128)(2,1)S(1)}, bf16[1024,1024]{1,0:T(8,128)(2,1)}, u32[]{:S(2)}, u32[]{:S(2)}) collective-permute-start(bf16[1024,1024]{1,0:T(8,128)(2,1)S(1)} %collective-permute-done.6.refs_4_.refs_5_), channel_id=1, source_target_pairs={{0,1},{1,0},{2,3},{3,2},{4,5},{5,4},{6,7},{7,6},{8,9},{9,8},{10,11... | collective-permute-start | bytes 6291464 | tf_op jit(solution)/shard_map/ppermute | solution.py:25
  106.0 27.1 %copy-start.9 = (bf16[512]{0:T(512)(128)(2,1)S(1)}, bf16[512]{0:T(512)(128)(2,1)}, u32[]{:S(2)}) copy-start(bf16[512]{0:T(512)(128)(2,1)} %param.21) | copy-start | bytes 3076
  106.0 25.9 %collective-permute-start.12 = (bf16[512,1024]{1,0:T(8,128)(2,1)}, bf16[512,1024]{1,0:T(8,128)(2,1)S(1)}, u32[]{:S(2)}, u32[]{:S(2)}) collective-permute-start(bf16[512,1024]{1,0:T(8,128)(2,1)} %slice.20), channel_id=1, source_target_pairs={{0,2},{1,3},{2,4},{3,5},{4,6},{5,7},{6,0},{7,1},{8,10},{9,11},{10,... | collective-permute-start | bytes 3145736 | tf_op jit(solution)/shard_map/ppermute | solution.py:21
  106.5 25.4 %collective-permute-start.13 = (bf16[512,1024]{1,0:T(8,128)(2,1)}, bf16[512,1024]{1,0:T(8,128)(2,1)}, u32[]{:S(2)}, u32[]{:S(2)}) collective-permute-start(bf16[512,1024]{1,0:T(8,128)(2,1)} %slice.21), channel_id=1, source_target_pairs={{0,6},{1,7},{2,0},{3,1},{4,2},{5,3},{6,4},{7,5},{8,14},{9,15},{10,... | collective-permute-start | bytes 3145736 | tf_op jit(solution)/shard_map/ppermute | solution.py:21
  132.0 16.1 %copy-start.6 = (bf16[512,1024]{1,0:T(8,128)(2,1)}, bf16[512,1024]{1,0:T(8,128)(2,1)S(1)}, u32[]{:S(2)}) copy-start(bf16[512,1024]{1,0:T(8,128)(2,1)S(1)} %collective-permute-done.12.refs_1_) | copy-start | bytes 3145732
  132.0 16.1 %collective-permute-start.16 = (bf16[512,1024]{1,0:T(8,128)(2,1)S(1)}, bf16[512,1024]{1,0:T(8,128)(2,1)S(1)}, u32[]{:S(2)}, u32[]{:S(2)}) collective-permute-start(bf16[512,1024]{1,0:T(8,128)(2,1)S(1)} %collective-permute-done.12.refs_1_), channel_id=1, source_target_pairs={{0,1},{1,0},{2,3},{3,2},{4,5},{5,4},{6,7},{7,6},{8,9},{9,8},{10,11... | collective-permute-start | bytes 3145736 | tf_op jit(solution)/shard_map/ppermute | solution.py:25
  133.0 15.1 %collective-permute-start.17 = (bf16[512,1024]{1,0:T(8,128)(2,1)}, bf16[512,1024]{1,0:T(8,128)(2,1)}, u32[]{:S(2)}, u32[]{:S(2)}) collective-permute-start(bf16[512,1024]{1,0:T(8,128)(2,1)} %collective-permute-done.13.refs_3_), channel_id=1, source_target_pairs={{0,1},{1,0},{2,3},{3,2},{4,5},{5,4},{6,7},{7,6},{8,9},{9,8},{10,11... | collective-permute-start | bytes 3145736 | tf_op jit(solution)/shard_map/ppermute | solution.py:25
  133.2 15.9 %copy-start = (f32[1024,128]{1,0:T(8,128)S(1)}, f32[1024,128]{1,0:T(8,128)}, u32[]{:S(2)}) copy-start(f32[1024,128]{1,0:T(8,128)} %shard_map.123.refs_6_) | copy-start | bytes 1572868
  148.1 1.0 copy-start.7
  159.9 2.0 %collective-permute-start.18 = (f32[8,1024]{1,0:T(8,128)S(1)}, f32[8,1024]{1,0:T(8,128)S(1)}, u32[]{:S(2)}, u32[]{:S(2)}) collective-permute-start(f32[8,1024]{1,0:T(8,128)S(1)} %shard_map.125), channel_id=1, source_target_pairs={{0,1},{1,0},{2,3},{3,2},{4,5},{5,4},{6,7},{7,6},{8,9},{9,8},{10,11... | collective-permute-start | bytes 98312 | tf_op jit(solution)/shard_map/ppermute | solution.py:25
  161.9 4.8 %collective-permute-start.19 = (f32[8,1024]{1,0:T(8,128)S(1)}, f32[8,1024]{1,0:T(8,128)S(1)}, u32[]{:S(2)}, u32[]{:S(2)}) collective-permute-start(f32[8,1024]{1,0:T(8,128)S(1)} %add.18), channel_id=1, source_target_pairs={{0,2},{1,3},{2,4},{3,5},{4,6},{5,7},{6,0},{7,1},{8,10},{9,11},{10,... | collective-permute-start | bytes 98312 | tf_op jit(solution)/shard_map/ppermute | solution.py:21
  163.1 4.4 %collective-permute-start.20 = (f32[8,1024]{1,0:T(8,128)S(1)}, f32[8,1024]{1,0:T(8,128)S(1)}, u32[]{:S(2)}, u32[]{:S(2)}) collective-permute-start(f32[8,1024]{1,0:T(8,128)S(1)} %add.18), channel_id=1, source_target_pairs={{0,4},{1,5},{2,6},{3,7},{4,0},{5,1},{6,2},{7,3},{8,12},{9,13},{10,... | collective-permute-start | bytes 98312 | tf_op jit(solution)/shard_map/ppermute | solution.py:21
  165.5 3.1 %collective-permute-start.21 = (f32[8,1024]{1,0:T(8,128)S(1)}, f32[8,1024]{1,0:T(8,128)S(1)}, u32[]{:S(2)}, u32[]{:S(2)}) collective-permute-start(f32[8,1024]{1,0:T(8,128)S(1)} %add.18), channel_id=1, source_target_pairs={{0,6},{1,7},{2,0},{3,1},{4,2},{5,3},{6,4},{7,5},{8,14},{9,15},{10,... | collective-permute-start | bytes 98312 | tf_op jit(solution)/shard_map/ppermute | solution.py:21
Sparse Core Ops, SparseCore 0:
  10.6 123.1 all-gather.1
